TPU v7x, 256 devices: a whole 4x4x8 slice. The times are simulated.
256 devices in a mesh: space: 16 (over z, y_lo), snap: 16 (over y_hi, x, core).
Axes of the slice: x: 4, y: 4 (y_hi: 2, y_lo: 2; y = y_hi * 2 + y_lo), z: 8, core: 2. Of those that a mesh axis runs over, the one named last changes fastest.
Arguments:
- primal: bfloat16 [2048, 196608], P('snap', 'space'), may hold values from -6 to 6
- adjoint_pencils: bfloat16 [1024, 196608], P('snap', 'space'), may hold values from -0.01953125 to 0.01953125
- weights: float32 [196608], P('space'), may hold values from 0.2 to 2
- pencil_map: int32 [1536], replicated, may hold values from 0 to 1535, as said below
Outputs:
- hankel: float32 [1024, 2048], P('space', 'snap')
Inputs may be any that keep to these rules, and one draw needn't show every extreme that they name: `pencil_map`: each number appears once; each aligned block of 96 entries holds exactly 6 entries from every aligned range of 96 values.
All inputs are finite; a program needn't handle non-finite values.
Results may differ from a plain program's by a relative error of at most 0.0029.
Values may be sent and summed in bfloat16 or wider, within the bound.
A program may use at most 128 MiB of HBM per device.

v0:
```python
import jax
import jax.numpy as jnp
from jax import lax
from jax.sharding import PartitionSpec as P

PEN_LEN = 128


def on_device(primal, adjoint_pencils, weights, pencil_map):
    rows_here = adjoint_pencils.shape[0]
    points = adjoint_pencils.shape[1]
    pen_dev = points // PEN_LEN
    tiles = lax.axis_size("space")
    share = pen_dev // tiles
    place = lax.axis_index("space")
    weighted = (primal.astype(jnp.float32) * weights[None, :]).astype(jnp.bfloat16)
    all_slots = pencil_map.reshape(tiles, pen_dev)
    targets = all_slots // pen_dev
    orders = jnp.argsort(targets, axis=1, stable=True)
    own_order = lax.dynamic_index_in_dim(orders, place, 0, keepdims=False)
    chosen = lax.dynamic_slice_in_dim(orders, place * share, share, 1)
    arrived = (jnp.take_along_axis(all_slots, chosen, axis=1) - place * pen_dev).reshape(pen_dev)
    blocks = adjoint_pencils.reshape(rows_here, pen_dev, PEN_LEN)
    outgoing = jnp.take(blocks, own_order, axis=1).reshape(rows_here, tiles, share, PEN_LEN)
    incoming = lax.all_to_all(outgoing, "space", split_axis=1, concat_axis=1, tiled=True)
    inverse = jnp.argsort(arrived)
    moving = jnp.take(incoming.reshape(rows_here, pen_dev, PEN_LEN), inverse, axis=1).reshape(
        rows_here, points
    )
    product = lax.dot_general(
        lax.all_gather(moving, "snap", axis=0, tiled=True),
        weighted,
        (((1,), (1,)), ((), ())),
        preferred_element_type=jnp.float32,
    )
    return lax.psum_scatter(product, "space", scatter_dimension=0, tiled=True)


def solution(mesh):
    placed = (P("snap", "space"), P("snap", "space"), P("space"), P())
    return jax.shard_map(
        on_device, mesh=mesh, in_specs=placed, out_specs=P("space", "snap"), check_vma=False
    )
```

profile of v0, /device:TPU:2, one launch (start us, length us, event | category | flops | bytes accessed | tf_op | source)
XLA Modules:
  0.0 308.6 jit_solution(8084344282338904994)
XLA Ops:
  6.5 0.9 reshape.38
  7.4 0.1 copy.12
  7.5 1.5 sort.34
  9.1 0.2 dynamic-slice_reduce_fusion
  9.3 0.4 copy_bitcast_fusion.1
  9.7 2.0 gather_fusion.1
  11.7 2.8 broadcast_select_fusion
  14.5 9.6 %all-to-all-start = ((bf16[64,16,6,128]{3,0,2,1:T(8,128)(2,1)}), bf16[64,16,6,128]{3,0,2,1:T(8,128)(2,1)S(1)}, u32[]{:S(2)}, u32[]{:S(2)}) async-start(bf16[64,16,6,128]{3,0,2,1:T(8,128)(2,1)} %bitcast.21), calls=%async_computation | async-start | bytes 3145728 | tf_op jit(solution)/shard_map/all_to_all | solution.py:25
  24.1 0.0 all-gather.2.cloned.1.call-start
  24.1 0.1 copy.13
  24.2 0.1 reshape.59
  24.3 1.2 gather_fusion
  25.6 0.1 reshape.62
  25.6 0.1 copy.14
  25.7 0.1 copy.15
  25.8 0.1 sub.19
  25.9 2.5 sort.35
  28.5 35.2 %all-to-all-done = bf16[64,16,6,128]{3,0,2,1:T(8,128)(2,1)S(1)} async-done(((bf16[64,16,6,128]{3,0,2,1:T(8,128)(2,1)}), bf16[64,16,6,128]{3,0,2,1:T(8,128)(2,1)S(1)}, u32[]{:S(2)}, u32[]{:S(2)}) %all-to-all-start) | async-done | bytes 1572896 | tf_op jit(solution)/shard_map/all_to_all | solution.py:25
  63.7 2.0 gather_fusion.2
  65.6 3.0 copy_bitcast_fusion
  68.6 0.0 reduce-scatter.2.cloned.1.call-start
  68.7 149.4 %all-gather.2.cloned.1.call-done = bf16[1024,12288]{1,0:T(8,128)(2,1)} async-done(((bf16[64,12288]{1,0:T(8,128)(2,1)}), bf16[1024,12288]{1,0:T(8,128)(2,1)}) %all-gather.2.cloned.1.call-update) | async-done | bytes 25165840 | tf_op jit(solution)/shard_map/all_gather | solution.py:31
  218.1 13.2 %fusion = f32[1024,128]{1,0:T(8,128)} fusion(bf16[1024,12288]{1,0:T(8,128)(2,1)} %all-gather.2.cloned.1.call-done, bf16[128,12288]{1,0:T(8,128)(2,1)} %param.6, f32[12288]{0:T(1024)S(1)} %copy-done.1), kind=kOutput, calls=%fused_computation.4 | convolution fusion | flops 3225944064 | bytes 28884992 | tf_op jit(solution)/shard_map/dot_general | solution.py:30
  231.3 70.5 %reduce-scatter.2.cloned.1.call-done = f32[64,128]{1,0:T(8,128)} async-done(((f32[1024,128]{1,0:T(8,128)}), f32[64,128]{1,0:T(8,128)}) %reduce-scatter.2.cloned.1.call-update) | async-done | bytes 32784 | tf_op jit(solution)/shard_map/reduce_scatter | solution.py:36
  (17 shorter events, 0.1 us)
Async XLA Ops:
  6.5 2.7 copy-start
  14.5 49.2 %all-to-all-start = ((bf16[64,16,6,128]{3,0,2,1:T(8,128)(2,1)}), bf16[64,16,6,128]{3,0,2,1:T(8,128)(2,1)S(1)}, u32[]{:S(2)}, u32[]{:S(2)}) async-start(bf16[64,16,6,128]{3,0,2,1:T(8,128)(2,1)} %bitcast.21), calls=%async_computation | async-start | bytes 3145728 | tf_op jit(solution)/shard_map/all_to_all | solution.py:25
  24.1 194.1 %all-gather.2.cloned.1.call-start = ((), (), s32[]{:S(2)}) async-start(), calls=%async_computation.2 | async-start | bytes 26738688 | tf_op jit(solution)/shard_map/all_gather | solution.py:31
  68.6 149.5 %copy-start.1 = (f32[12288]{0:T(1024)S(1)}, f32[12288]{0:T(1024)}, u32[]{:S(2)}) copy-start(f32[12288]{0:T(1024)} %param.8) | copy-start | bytes 147460
  68.6 233.2 %reduce-scatter.2.cloned.1.call-start = ((), (), s32[]{:S(2)}) async-start(), calls=%async_computation.3 | async-start | bytes 557056 | tf_op jit(solution)/shard_map/reduce_scatter | solution.py:36
Sparse Core Ops, SparseCore 0:
  68.8 149.3 all-gather.1
  231.4 70.3 reduce-scatter.1
where the time goes:
time: 309 us
  waiting for transfers between devices  255 us (83%)
  between operations  13.5 us (4%)
  matrix products  13.2 us (4%)
  other arithmetic  9.89 us (3%)
  starting transfers between devices  9.67 us (3%)
  local copies, waits for them, and re-layouts  7.27 us (2%)
    all_gather x1, waiting for transfers between devices, on_device(): lax.all_gather(moving, 'snap', axis=0, tiled=True)  149 us
    reduce_scatter x1, waiting for transfers between devices, on_device(): return lax.psum_scatter(product, 'space', scatter_dimension=0, tiled=True)  70.5 us
    all_to_all x1, waiting for transfers between devices, on_device(): lax.all_to_all(outgoing, 'space', split_axis=1, concat_axis=1, tiled=True)  35.2 us
    dot_general x1, matrix products, on_device(): lax.dot_general(lax.all_gather(moving, 'snap', axis=0, tiled=True), weigh...  13.2 us
    all_to_all x1, starting transfers between devices, on_device(): lax.all_to_all(outgoing, 'space', split_axis=1, concat_axis=1, tiled=True)  9.58 us
  transfers between devices with their start and end apart: 3, of which 3 were waited for; matrix products, arithmetic and copies ran while one was open for 1% of the time, Pallas kernels for 0%

commit v1 on v0

v1 whole, which is shorter than its diff:
```python
import functools
import jax
import jax.numpy as jnp
from jax import lax
from jax.experimental import pallas as pl
from jax.experimental.pallas import tpu as pltpu
from jax.sharding import PartitionSpec as P

PEN = 128
NX, NZ = 4, 8
TILES = 16
DEV_PEN = 96
SHARE = 6
MESH = pl.DeviceIdType.MESH
BLK = SHARE * PEN
KLOC = 4 * BLK


def where_am_i():
    space = lax.axis_index("space")
    snap = lax.axis_index("snap")
    return space // 2, space % 2, snap // 8, (snap // 2) % NX, snap % 2


def device(z, ylo, yh, x, c):
    return {"space": z * 2 + ylo, "snap": yh * 8 + x * 2 + c}


def sort_kernel(pos_a, pos_p, a_ref, p_ref, w_ref, as_ref, ps_ref):
    for i in range(DEV_PEN):
        at = pos_a[0, i]
        lane = pl.ds(pl.multiple_of((at % SHARE) * PEN, PEN), PEN)
        as_ref[at // SHARE, :, lane] = a_ref[:, i * PEN:(i + 1) * PEN]
    for i in range(DEV_PEN):
        at = pos_p[0, i]
        lane = pl.ds(pl.multiple_of((at % 24) * PEN, PEN), PEN)
        span = slice(i * PEN, (i + 1) * PEN)
        ps_ref[at // 24, :, lane] = (p_ref[:, span].astype(jnp.float32) * w_ref[:, span]).astype(jnp.bfloat16)


def sort_local(primal, adjoint, weights, pencil_map):
    z, ylo, _, _, _ = where_am_i()
    space = lax.axis_index("space")
    maps = pencil_map.reshape(TILES, DEV_PEN)
    target = maps // DEV_PEN
    before = jnp.arange(DEV_PEN)[None, :] < jnp.arange(DEV_PEN)[:, None]
    rank = jnp.sum((target[:, :, None] == target[:, None, :]) & before[None], axis=2, dtype=jnp.int32)
    own_target = lax.dynamic_index_in_dim(target, space, 0, keepdims=False)
    own_rank = lax.dynamic_index_in_dim(rank, space, 0, keepdims=False)
    dz_a = (own_target // 2 - z) % NZ
    pos_a = (dz_a * 2 + own_target % 2) * SHARE + own_rank
    src = jnp.arange(TILES, dtype=jnp.int32)
    dz_p = (z - src // 2) % NZ
    base = (dz_p % NX) * 24 + (dz_p // NX) * 12 + (src % 2) * SHARE
    place = base[:, None] + rank
    slots = space * DEV_PEN + jnp.arange(DEV_PEN, dtype=jnp.int32)
    pos_p = jnp.sum(jnp.where(maps[None] == slots[:, None, None], place[None], 0), axis=(1, 2), dtype=jnp.int32)
    rows_a, points = adjoint.shape
    rows_p = primal.shape[0]
    steps = 4
    return pl.pallas_call(
        sort_kernel,
        grid=(steps,),
        in_specs=[
            pl.BlockSpec(memory_space=pltpu.SMEM),
            pl.BlockSpec(memory_space=pltpu.SMEM),
            pl.BlockSpec((rows_a // steps, points), lambda i: (i, 0)),
            pl.BlockSpec((rows_p // steps, points), lambda i: (i, 0)),
            pl.BlockSpec((1, points), lambda i: (0, 0)),
        ],
        out_specs=[
            pl.BlockSpec((TILES, rows_a // steps, BLK), lambda i: (0, i, 0)),
            pl.BlockSpec((NX, rows_p // steps, KLOC), lambda i: (0, i, 0)),
        ],
        out_shape=[
            jax.ShapeDtypeStruct((TILES, rows_a, BLK), jnp.bfloat16),
            jax.ShapeDtypeStruct((NX, rows_p, KLOC), jnp.bfloat16),
        ],
        name="sort_local",
    )(pos_a[None], pos_p[None], adjoint, primal, weights[None])


ORDER = (0, 1, 7, 2, 6, 3, 5, 4)


def main_kernel(as_ref, ps_ref, o_ref, r1, afin, pfin, own, psend, rx, tot, r2,
                ss1, rs1, ssp, rsp, ssy, rsy, ssc, rsc, ssx, rsx, ss2, rs2):
    z, ylo, yh, x, c = where_am_i()
    space = z * 2 + ylo

    def remote(src, dst, ss, rs, dev):
        return pltpu.make_async_remote_copy(src_ref=src, dst_ref=dst, send_sem=ss, recv_sem=rs,
                                            device_id=dev, device_id_type=MESH)

    bar = pltpu.get_barrier_semaphore()

    def greet(dev):
        pl.semaphore_signal(bar, inc=1, device_id=dev, device_id_type=MESH)

    for zi in range(2):
        for xs in range(NX):
            dev = device((z - x - 4 * zi + 2 * NZ) % NZ, ylo, yh, xs, c)
            if zi == 0 and xs == 0:
                @pl.when(x != 0)
                def _():
                    greet(dev)
            else:
                greet(dev)
    for d in range(1, NX):
        greet(device(z, ylo, yh, (x + d) % NX, c))
    greet(device(z, ylo, 1 - yh, x, c))
    greet(device(z, 1 - ylo, 0, x, c))
    greet(device(z, 1 - ylo, 1, x, c))
    greet(device(z, ylo, yh, x, 1 - c))
    for d in range(1, TILES):
        to = (space + d) % TILES
        greet(device(to // 2, to % 2, yh, x, c))
    pl.semaphore_wait(bar, 7 + 3 + 3 + 1 + 15 + (x + NX - 1) // NX)

    def a_copy(dz):
        return remote(as_ref.at[pl.ds(dz * 2, 2)], r1.at[dz // NX, x], ss1.at[dz], rs1.at[dz // NX, x],
                      device((z + dz) % NZ, ylo, yh, dz % NX, c))

    local_a = pltpu.make_async_copy(as_ref.at[pl.ds(0, 2)], r1.at[0, 0], rs1.at[0, 0])
    for dz in ORDER:
        if dz == 0:
            @pl.when(x == 0)
            def _():
                local_a.start()

            @pl.when(x != 0)
            def _():
                a_copy(0).start()
        else:
            a_copy(dz).start()

    own_p = pltpu.make_async_copy(ps_ref.at[x], pfin.at[0], rsp.at[0])
    own_p.start()
    p_copies = []
    for d in (1, 3, 2):
        cp = remote(ps_ref.at[(x + d) % NX], pfin.at[(NX - d)], ssp.at[d - 1], rsp.at[NX - d],
                    device(z, ylo, yh, (x + d) % NX, c))
        cp.start()
        p_copies.append(cp)

    chunks = [(zi, d) for zi in range(2) for d in range(NX)]

    def y_copies(k, local=True):
        zi, d = chunks[k]
        xs = (x + d) % NX
        rb = yh * 8 + xs * 2 + c
        dst = afin.at[rb, :, pl.ds(pl.multiple_of((zi * 2 + ylo) * BLK, BLK), BLK)]
        mine = r1.at[zi, xs, ylo]
        other = r1.at[zi, xs, 1 - ylo]
        rs = rsy.at[yh, xs, zi, ylo]
        out = [
            remote(other, dst, ssy.at[k, 0], rs, device(z, 1 - ylo, yh, x, c)),
            remote(other, dst, ssy.at[k, 1], rs, device(z, 1 - ylo, 1 - yh, x, c)),
            remote(mine, dst, ssy.at[k, 2], rs, device(z, ylo, 1 - yh, x, c)),
        ]
        return out + ([pltpu.make_async_copy(mine, dst, rs)] if local else [])

    def blocks(k, core):
        zi, d = chunks[k]
        xs = (x + d) % NX
        for dy in range(2):
            for dl in range(2):
                ys, ls = (yh + dy) % 2, (ylo + dl) % 2
                rb = ys * 8 + xs * 2 + core
                blk = afin.at[rb, :, pl.ds(pl.multiple_of((zi * 2 + ls) * BLK, BLK), BLK)]
                yield blk, (ys, xs, zi, ls), (k, dy, dl)

    def c_copies(k):
        return [remote(blk, blk, ssc.at[send], rsc.at[at], device(z, ylo, yh, x, 1 - c))
                for blk, at, send in blocks(k, c)]

    lag = 2
    for k in range(len(chunks) + lag):
        if k < len(chunks):
            zi, d = chunks[k]
            xs = (x + d) % NX
            pltpu.make_async_copy(as_ref.at[pl.ds(0, 2)], r1.at[zi, xs], rs1.at[zi, xs]).wait()
            for cp in y_copies(k):
                cp.start()
        if k >= lag:
            for (blk, at, _), cp in zip(blocks(k - lag, c), c_copies(k - lag)):
                pltpu.make_async_copy(blk, blk, rsy.at[at]).wait()
                cp.start()
    for k in range(len(chunks)):
        for blk, at, _ in blocks(k, 1 - c):
            pltpu.make_async_copy(blk, blk, rsc.at[at]).wait()

    rows_mm = 256

    def product(slot, put):
        def body(i, carry):
            at = pl.multiple_of(i * (rows_mm // 64), rows_mm // 64)
            a = afin[pl.ds(at, rows_mm // 64)].reshape(rows_mm, KLOC)
            put(pl.multiple_of(i * rows_mm, rows_mm), lax.dot_general(
                a, pfin[slot], (((1,), (1,)), ((), ())), preferred_element_type=jnp.float32))
            return carry
        lax.fori_loop(0, 1024 // rows_mm, body, 0)

    def put_own(row, v):
        own[pl.ds(row, rows_mm), :] = v

    x_copies = []
    own_p.wait()
    product(0, put_own)
    for d in (1, 3, 2):
        pltpu.make_async_copy(ps_ref.at[0], pfin.at[d], rsp.at[d]).wait()

        def put_send(row, v, d=d):
            psend[d - 1, pl.ds(row, rows_mm), :] = v.astype(psend.dtype)
        product(d, put_send)
        cp = remote(psend.at[d - 1], rx.at[NX - d - 1], ssx.at[d - 1], rsx.at[NX - d - 1],
                    device(z, ylo, yh, (x + d) % NX, c))
        cp.start()
        x_copies.append(cp)

    for d in range(1, NX):
        pltpu.make_async_copy(psend.at[0], rx.at[d - 1], rsx.at[d - 1]).wait()
    tot[...] = (own[...] + rx[0].astype(jnp.float32) + rx[1].astype(jnp.float32)
                + rx[2].astype(jnp.float32)).reshape(tot.shape)

    f_copies = []
    for d in range(1, TILES):
        to = (space + d) % TILES
        cp = remote(tot.at[to], r2.at[TILES - d - 1], ss2.at[d - 1], rs2.at[TILES - d - 1],
                    device(to // 2, to % 2, yh, x, c))
        cp.start()
        f_copies.append(cp)
    acc = tot[space]
    for d in range(1, TILES):
        pltpu.make_async_copy(tot.at[0], r2.at[d - 1], rs2.at[d - 1]).wait()
        acc = acc + r2[d - 1]
    o_ref[...] = acc

    @pl.when(x != 0)
    def _():
        a_copy(0).wait_send()
    for dz in range(1, NZ):
        a_copy(dz).wait_send()
    for cp in p_copies + x_copies + f_copies:
        cp.wait_send()
    for k in range(len(chunks)):
        for cp in y_copies(k, local=False):
            cp.wait_send()
        for cp in c_copies(k):
            cp.wait_send()


def exchange(a_sorted, p_sorted):
    bf, f32 = jnp.bfloat16, jnp.float32
    dma = pltpu.SemaphoreType.DMA
    return pl.pallas_call(
        main_kernel,
        in_specs=[pl.BlockSpec(memory_space=pl.ANY)] * 2,
        out_specs=pl.BlockSpec(memory_space=pltpu.VMEM),
        out_shape=jax.ShapeDtypeStruct((64, 128), f32),
        scratch_shapes=[
            pltpu.VMEM((2, NX, 2, 64, BLK), bf),
            pltpu.VMEM((16, 64, KLOC), bf),
            pltpu.VMEM((NX, 128, KLOC), bf),
            pltpu.VMEM((1024, 128), f32),
            pltpu.VMEM((3, 1024, 128), bf),
            pltpu.VMEM((3, 1024, 128), bf),
            pltpu.VMEM((TILES, 64, 128), f32),
            pltpu.VMEM((TILES - 1, 64, 128), f32),
            dma((NZ,)), dma((2, NX)),
            dma((3,)), dma((NX,)),
            dma((8, 3)), dma((2, NX, 2, 2)),
            dma((8, 2, 2)), dma((2, NX, 2, 2)),
            dma((3,)), dma((3,)),
            dma((TILES - 1,)), dma((TILES - 1,)),
        ],
        compiler_params=pltpu.CompilerParams(
            collective_id=0, has_side_effects=True, vmem_limit_bytes=48 * 1024 * 1024),
        name="exchange",
    )(a_sorted, p_sorted)


def on_device(primal, adjoint_pencils, weights, pencil_map):
    a_sorted, p_sorted = sort_local(primal, adjoint_pencils, weights, pencil_map)
    return exchange(a_sorted, p_sorted)


def solution(mesh):
    placed = (P("snap", "space"), P("snap", "space"), P("space"), P())
    return jax.shard_map(
        on_device, mesh=mesh, in_specs=placed, out_specs=P("space", "snap"), check_vma=False
    )
```

time: 309 us -> 126 us (0.41)
  waiting for transfers between devices: 255 us -> 0 us
  Pallas kernels: 0 us -> 117 us
  between operations: 13.5 us -> 0.03 us
  matrix products: 13.2 us -> 0 us
  starting transfers between devices: 9.67 us -> 0 us
  other arithmetic: 9.89 us -> 3.63 us
    all_gather x1 -> x0, waiting for transfers between devices: 149 us -> none  [on_device(): lax.all_gather(moving, 'snap', axis=0, tiled=True)]
    pallas_call x0 -> x2, Pallas kernels: none -> 117 us  [the longest x1 108 us: exchange(): pl.pallas_call(main_kernel, in_specs=[pl.BlockSpec(memory_space=pl.ANY)]...]
    reduce_scatter x1 -> x0, waiting for transfers between devices: 70.5 us -> none  [on_device(): return lax.psum_scatter(product, 'space', scatter_dimension=0, tiled=True)]
    all_to_all x1 -> x0, waiting for transfers between devices: 35.2 us -> none  [on_device(): lax.all_to_all(outgoing, 'space', split_axis=1, concat_axis=1, tiled=True)]
    dot_general x1 -> x0, matrix products: 13.2 us -> none  [on_device(): lax.dot_general(lax.all_gather(moving, 'snap', axis=0, tiled=True), weigh...]
    all_to_all x1 -> x0, starting transfers between devices: 9.58 us -> none  [on_device(): lax.all_to_all(outgoing, 'space', split_axis=1, concat_axis=1, tiled=True)]
    gather x7 -> x0, local copies, waits for them, and re-layouts: 5.49 us -> none  [the longest x1 1.96 us: on_device(): jnp.take(blocks, own_order, axis=1)]
    sort x2 -> x0, other arithmetic: 4.05 us -> none  [the longest x1 2.54 us: on_device(): inverse = jnp.argsort(arrived)]
  transfers between devices with their start and end apart: 3 -> 0, of which waited for: 3 -> 0; matrix products, arithmetic and copies ran while one was open for 1% -> 0% of each run, Pallas kernels for 0% -> 0%
where the time goes in v1:
time: 126 us; the launch traced here: 125 us
  Pallas kernels  117 us (93%)
  local copies, waits for them, and re-layouts  4.68 us (4%)
  other arithmetic  3.63 us (3%)
    pallas_call x1, Pallas kernels, exchange(): pl.pallas_call(main_kernel, in_specs=[pl.BlockSpec(memory_space=pl.ANY)]...  108 us
    pallas_call x1, Pallas kernels, sort_local(): pl.pallas_call(sort_kernel, grid=(steps,), in_specs=[pl.BlockSpec(memory_...  8.41 us
    unnamed x5, local copies, waits for them, and re-layouts  3.91 us

profile of v1, /device:TPU:2, one launch (start us, length us, event | category | flops | bytes accessed | tf_op | source)
XLA Modules:
  0.0 125.2 jit_solution(6846847189045949957)
XLA Ops:
  0.0 0.8 reshape.134
  0.8 0.6 convert_reduce_fusion
  1.4 0.5 dynamic-slice_add_fusion.pos_a
  2.0 0.1 broadcast_add_fusion
  2.0 2.4 %select_reduce_fusion = s32[96]{0:T(128)} fusion(s32[16,96]{1,0:T(8,128)S(1)} %broadcast_add_fusion, s32[16,96]{1,0:T(8,128)S(1)} %reshape.134, s32[96]{0:T(128)S(1)} %iota_add_fusion), kind=kLoop, calls=%fused_computation | loop fusion | flops 442272 | bytes 13056 | tf_op jit(solution)/shard_map/reduce_sum | solution.py:57
  4.4 8.4 %sort_local.1 = (bf16[16,64,768]{2,1,0:T(8,128)(2,1)}, bf16[4,128,3072]{2,1,0:T(8,128)(2,1)}) custom-call(s32[1,96]{1,0:T(1,128)} %dynamic-slice_add_fusion.pos_a, s32[1,96]{1,0:T(1,128)} %bitcast.3, bf16[64,12288]{1,0:T(8,128)(2,1)} %a_ref.1, bf16[128,12288]{1,0:T(8,128)(2,1)} %p_ref.1, f32[1,12288]{1,0:T(1,128)} %bitcast.2), custom_call_target="tpu_custom_call" | custom-call | tf_op jit(solution)/shard_map/sort_local/pallas_call | solution.py:61
  12.8 0.0 copy-start
  12.8 1.9 %copy-done = bf16[4,128,3072]{2,1,0:T(8,128)(2,1)S(1)} copy-done((bf16[4,128,3072]{2,1,0:T(8,128)(2,1)S(1)}, bf16[4,128,3072]{2,1,0:T(8,128)(2,1)}, u32[]{:S(2)}) %copy-start) | copy-done | bytes 3145752
  14.7 0.0 copy-start.1
  14.7 1.4 %copy-done.1 = bf16[16,64,768]{2,1,0:T(8,128)(2,1)S(1)} copy-done((bf16[16,64,768]{2,1,0:T(8,128)(2,1)S(1)}, bf16[16,64,768]{2,1,0:T(8,128)(2,1)}, u32[]{:S(2)}) %copy-start.1) | copy-done | bytes 1572888
  16.1 108.4 %exchange.1 = f32[64,128]{1,0:T(8,128)S(1)} custom-call(bf16[16,64,768]{2,1,0:T(8,128)(2,1)S(1)} %copy-done.1, bf16[4,128,3072]{2,1,0:T(8,128)(2,1)S(1)} %copy-done), custom_call_target="tpu_custom_call" | custom-call | tf_op jit(solution)/shard_map/exchange/pallas_call | solution.py:256
  124.6 0.6 copy.6
  (4 shorter events, 0.1 us)
Async XLA Ops:
  12.8 1.9 %copy-start = (bf16[4,128,3072]{2,1,0:T(8,128)(2,1)S(1)}, bf16[4,128,3072]{2,1,0:T(8,128)(2,1)}, u32[]{:S(2)}) copy-start(bf16[4,128,3072]{2,1,0:T(8,128)(2,1)} %get-tuple-element.8.ps_ref) | copy-start | bytes 9437188
  14.7 1.4 %copy-start.1 = (bf16[16,64,768]{2,1,0:T(8,128)(2,1)S(1)}, bf16[16,64,768]{2,1,0:T(8,128)(2,1)}, u32[]{:S(2)}) copy-start(bf16[16,64,768]{2,1,0:T(8,128)(2,1)} %get-tuple-element.7.as_ref) | copy-start | bytes 4718596

commit v2 on v0

v2 whole, which is shorter than its diff:
```python
import functools
import jax
import jax.numpy as jnp
from jax import lax
from jax.experimental import pallas as pl
from jax.experimental.pallas import tpu as pltpu
from jax.sharding import PartitionSpec as P

PEN = 128
NX, NZ = 4, 8
TILES = 16
DEV_PEN = 96
SHARE = 6
MESH = pl.DeviceIdType.MESH
BLK = SHARE * PEN
KLOC = 4 * BLK


def where_am_i():
    space = lax.axis_index("space")
    snap = lax.axis_index("snap")
    return space // 2, space % 2, snap // 8, (snap // 2) % NX, snap % 2


def device(z, ylo, yh, x, c):
    return {"space": z * 2 + ylo, "snap": yh * 8 + x * 2 + c}


ORDER = (0, 1, 7, 2, 6, 4, 3, 5)
XORDER = (1, 3, 2)
ROWS = 256
STEPS = 1024 // ROWS


def main_kernel(idx_a, idx_p, w_ref, a_hbm, p_hbm, o_ref, a_v, p_v, asort, psort, r1, afin, pfin,
                own, psend, rx, tot, r2,
                lsem, ss1, rs1, ssp, rsp, ssy, rsy, ssc, rsc, ssx, rsx, ss2, rs2):
    z, ylo, yh, x, c = where_am_i()
    space = z * 2 + ylo

    def remote(src, dst, ss, rs, dev):
        return pltpu.make_async_remote_copy(src_ref=src, dst_ref=dst, send_sem=ss, recv_sem=rs,
                                            device_id=dev, device_id_type=MESH)

    def arrived(ref, sem):
        pltpu.make_async_copy(ref, ref, sem).wait()

    def load(hbm, v, sem):
        def body(i, carry):
            lane = pl.ds(pl.multiple_of(i * PEN, PEN), PEN)
            pltpu.make_async_copy(hbm.at[:, lane], v.at[i], sem).start()
            return carry
        lax.fori_loop(0, DEV_PEN, body, 0)

    load(a_hbm, a_v, lsem.at[0])

    bar = pltpu.get_barrier_semaphore()

    def greet(dev):
        pl.semaphore_signal(bar, inc=1, device_id=dev, device_id_type=MESH)

    for zi in range(2):
        for xs in range(NX):
            dev = device((z - x - 4 * zi + 2 * NZ) % NZ, ylo, yh, xs, c)
            if zi == 0 and xs == 0:
                @pl.when(x != 0)
                def _():
                    greet(dev)
            else:
                greet(dev)
    for d in range(1, NX):
        greet(device(z, ylo, yh, (x + d) % NX, c))
    greet(device(z, ylo, 1 - yh, x, c))
    greet(device(z, 1 - ylo, 0, x, c))
    greet(device(z, 1 - ylo, 1, x, c))
    greet(device(z, ylo, yh, x, 1 - c))
    for d in range(1, TILES):
        to = (space + d) % TILES
        greet(device(to // 2, to % 2, yh, x, c))

    load(p_hbm, p_v, lsem.at[1])

    arrived(a_v, lsem.at[0])
    for dz in range(NZ):
        for lt in range(2):
            t = ((z + dz) % NZ) * 2 + lt
            for r in range(SHARE):
                asort[dz, lt, :, r * PEN:(r + 1) * PEN] = a_v[idx_a[t, r]]

    pl.semaphore_wait(bar, 7 + 3 + 3 + 1 + 15 + (x + NX - 1) // NX)

    def a_copy(dz, l):
        lt = (1 - ylo + l) % 2
        return remote(asort.at[dz, lt], r1.at[dz // NX, x, lt], ss1.at[dz, l], rs1.at[dz // NX, x, lt],
                      device((z + dz) % NZ, ylo, yh, dz % NX, c))

    for dz in ORDER:
        for l in range(2):
            if dz == 0:
                lt = (1 - ylo + l) % 2

                @pl.when(x == 0)
                def _():
                    pltpu.make_async_copy(asort.at[0, lt], r1.at[0, 0, lt], rs1.at[0, 0, lt]).start()

                @pl.when(x != 0)
                def _():
                    a_copy(0, l).start()
            else:
                a_copy(dz, l).start()

    def p_copy(slot):
        d = XORDER[slot - 1]
        return remote(psort.at[d], pfin.at[XORDER.index(NX - d) + 1], ssp.at[slot - 1],
                      rsp.at[XORDER.index(NX - d) + 1], device(z, ylo, yh, (x + d) % NX, c))

    own_p = pltpu.make_async_copy(psort.at[0], pfin.at[0], rsp.at[0])
    arrived(p_v, lsem.at[1])
    for step, d in enumerate(XORDER + (0,)):
        for zi in range(2):
            dz = (x + d) % NX + NX * zi
            for ls in range(2):
                src = ((z - dz + NZ) % NZ) * 2 + ls
                for r in range(SHARE):
                    i = idx_p[src, r]
                    at = ((zi * 2 + ls) * SHARE + r) * PEN
                    psort[d, :, at:at + PEN] = (
                        p_v[i].astype(jnp.float32) * w_ref[i]).astype(jnp.bfloat16)
        if step >= 1:
            p_copy(step).start()
    own_p.start()

    flip = x // 3
    chunks = [(j, d, l) for j in range(2) for d in (0, 1, 3, 2) for l in range(2)]

    def chunk(k):
        j, d, l = chunks[k]
        return (j + flip) % 2, (x + d) % NX, (1 - ylo + l) % 2

    def block(ys, xs, core, zi, ls):
        return afin.at[ys * 8 + xs * 2 + core, :, pl.ds(pl.multiple_of((zi * 2 + ls) * BLK, BLK), BLK)]

    def y_copies(k):
        zi, xs, lt = chunk(k)
        src = r1.at[zi, xs, lt]
        dst = block(yh, xs, c, zi, ylo)
        rs = rsy.at[yh, xs, zi, ylo]
        out = [remote(src, dst, ssy.at[k, 0], rs, device(z, lt, 1 - yh, x, c))]
        if chunks[k][2] == 0:
            out.append(remote(src, dst, ssy.at[k, 1], rs, device(z, lt, yh, x, c)))
        return out

    def sources(k):
        j, d, l = chunks[k]
        zi, xs = (j + flip) % 2, (x + d) % NX
        ls = (ylo + 1 - l) % 2
        return [((yh + dy) % 2, xs, zi, ls, dy) for dy in range(2)]

    def c_copies(k):
        return [remote(block(ys, xs, c, zi, ls), block(ys, xs, c, zi, ls), ssc.at[k, dy],
                       rsc.at[ys, xs, zi, ls], device(z, ylo, yh, x, 1 - c))
                for ys, xs, zi, ls, dy in sources(k)]

    lag = 4
    for k in range(len(chunks) + lag):
        if k < len(chunks):
            zi, xs, lt = chunk(k)
            arrived(r1.at[zi, xs, lt], rs1.at[zi, xs, lt])
            for cp in y_copies(k):
                cp.start()
            if chunks[k][2] == 1:
                pltpu.make_async_copy(r1.at[zi, xs, lt], block(yh, xs, c, zi, ylo),
                                      rsy.at[yh, xs, zi, ylo]).start()
        if k >= lag:
            for (ys, xs, zi, ls, _), cp in zip(sources(k - lag), c_copies(k - lag)):
                arrived(block(ys, xs, c, zi, ls), rsy.at[ys, xs, zi, ls])
                cp.start()
    for k in range(len(chunks)):
        for ys, xs, zi, ls, _ in sources(k):
            arrived(block(ys, xs, 1 - c, zi, ls), rsc.at[ys, xs, zi, ls])

    first = z // 2

    def rows_at(i):
        return (first + i) % STEPS

    def lhs(i):
        return afin[pl.ds(rows_at(i) * (ROWS // 64), ROWS // 64)].reshape(ROWS, KLOC)

    def times(a, b):
        return lax.dot_general(a, b, (((1,), (1,)), ((), ())), preferred_element_type=jnp.float32)

    def x_copy(slot, i):
        d = XORDER[slot - 1]
        back = XORDER.index(NX - d)
        return remote(psend.at[slot - 1, rows_at(i)], rx.at[back, rows_at(i)], ssx.at[slot - 1, i],
                      rsx.at[back, i], device(z, ylo, yh, (x + d) % NX, c))

    arrived(pfin.at[0], rsp.at[0])
    arrived(pfin.at[1], rsp.at[1])
    for i in range(STEPS):
        v = times(lhs(i), pfin[0:2].reshape(256, KLOC))
        own[rows_at(i)] = v[:, :128]
        psend[0, rows_at(i)] = v[:, 128:].astype(psend.dtype)
        x_copy(1, i).start()
    for slot in (2, 3):
        arrived(pfin.at[slot], rsp.at[slot])
        for i in range(STEPS):
            psend[slot - 1, rows_at(i)] = times(lhs(i), pfin[slot]).astype(psend.dtype)
            x_copy(slot, i).start()

    def f_copy(i, j):
        to = rows_at(i) * (ROWS // 64) + j
        return to, remote(tot.at[to], r2.at[space], ss2.at[i, j], rs2.at[space],
                          device(to // 2, to % 2, yh, x, c))

    for i in range(STEPS):
        at = rows_at(i)
        total = own[at]
        for slot in range(3):
            arrived(rx.at[slot, at], rsx.at[slot, i])
            total = total + rx[slot, at].astype(jnp.float32)
        tot[pl.ds(at * (ROWS // 64), ROWS // 64)] = total.reshape(ROWS // 64, 64, 128)
        for j in range(ROWS // 64):
            to = at * (ROWS // 64) + j

            @pl.when(to != space)
            def _():
                f_copy(i, j)[1].start()
    acc = tot[space]
    for d in range(1, TILES):
        frm = (space + d) % TILES
        arrived(r2.at[frm], rs2.at[frm])
        acc = acc + r2[frm]
    o_ref[...] = acc

    for l in range(2):
        @pl.when(x != 0)
        def _():
            a_copy(0, l).wait_send()
        for dz in range(1, NZ):
            a_copy(dz, l).wait_send()
    for slot in range(1, NX):
        p_copy(slot).wait_send()
        for i in range(STEPS):
            x_copy(slot, i).wait_send()
    for k in range(len(chunks)):
        for cp in y_copies(k) + c_copies(k):
            cp.wait_send()
    for i in range(STEPS):
        for j in range(ROWS // 64):
            to = rows_at(i) * (ROWS // 64) + j

            @pl.when(to != space)
            def _():
                f_copy(i, j)[1].wait_send()


def exchange(idx_a, idx_p, weights, adjoint, primal):
    bf, f32 = jnp.bfloat16, jnp.float32
    dma = pltpu.SemaphoreType.DMA
    smem = pl.BlockSpec(memory_space=pltpu.SMEM)
    hbm = pl.BlockSpec(memory_space=pl.ANY)
    vmem = pl.BlockSpec(memory_space=pltpu.VMEM)
    return pl.pallas_call(
        main_kernel,
        in_specs=[smem, smem, vmem, hbm, hbm],
        out_specs=vmem,
        out_shape=jax.ShapeDtypeStruct((64, 128), f32),
        scratch_shapes=[
            pltpu.VMEM((DEV_PEN, 64, PEN), bf),
            pltpu.VMEM((DEV_PEN, 128, PEN), bf),
            pltpu.VMEM((NZ, 2, 64, BLK), bf),
            pltpu.VMEM((NX, 128, KLOC), bf),
            pltpu.VMEM((2, NX, 2, 64, BLK), bf),
            pltpu.VMEM((16, 64, KLOC), bf),
            pltpu.VMEM((NX, 128, KLOC), bf),
            pltpu.VMEM((STEPS, ROWS, 128), f32),
            pltpu.VMEM((3, STEPS, ROWS, 128), bf),
            pltpu.VMEM((3, STEPS, ROWS, 128), bf),
            pltpu.VMEM((TILES, 64, 128), f32),
            pltpu.VMEM((TILES, 64, 128), f32),
            dma((2,)),
            dma((NZ, 2)), dma((2, NX, 2)),
            dma((3,)), dma((NX,)),
            dma((16, 2)), dma((2, NX, 2, 2)),
            dma((16, 2)), dma((2, NX, 2, 2)),
            dma((3, STEPS)), dma((3, STEPS)),
            dma((STEPS, ROWS // 64)), dma((TILES,)),
        ],
        compiler_params=pltpu.CompilerParams(
            collective_id=0, has_side_effects=True, vmem_limit_bytes=60 * 1024 * 1024),
        name="exchange",
    )(idx_a, idx_p, weights.reshape(DEV_PEN, 1, PEN), adjoint, primal)


def on_device(primal, adjoint_pencils, weights, pencil_map):
    space = lax.axis_index("space")
    maps = pencil_map.reshape(TILES, DEV_PEN)
    target = maps // DEV_PEN
    before = jnp.arange(DEV_PEN)[None, :] < jnp.arange(DEV_PEN)[:, None]
    rank = jnp.sum((target[:, :, None] == target[:, None, :]) & before[None], axis=2, dtype=jnp.int32)
    of_rank = jnp.arange(SHARE, dtype=jnp.int32)[None, :, None]
    here = (target == space)[:, None, :] & (rank[:, None, :] == of_rank)
    idx_p = jnp.sum(jnp.where(here, maps[:, None, :] - space * DEV_PEN, 0), axis=2, dtype=jnp.int32)
    own_target = lax.dynamic_index_in_dim(target, space, 0, keepdims=True)
    own_rank = lax.dynamic_index_in_dim(rank, space, 0, keepdims=True)
    to = (own_target == jnp.arange(TILES, dtype=jnp.int32)[:, None])[:, None, :] & (own_rank[:, None, :] == of_rank)
    idx_a = jnp.sum(jnp.where(to, jnp.arange(DEV_PEN, dtype=jnp.int32), 0), axis=2, dtype=jnp.int32)
    return exchange(idx_a, idx_p, weights, adjoint_pencils, primal)


def solution(mesh):
    placed = (P("snap", "space"), P("snap", "space"), P("space"), P())
    return jax.shard_map(
        on_device, mesh=mesh, in_specs=placed, out_specs=P("space", "snap"), check_vma=False
    )
```

time: 309 us -> 103 us (0.33)
  waiting for transfers between devices: 255 us -> 0 us
  Pallas kernels: 0 us -> 96.5 us
  between operations: 13.5 us -> 0.05 us
  matrix products: 13.2 us -> 0 us
  starting transfers between devices: 9.67 us -> 0 us
  other arithmetic: 9.89 us -> 2.4 us
  local copies, waits for them, and re-layouts: 7.27 us -> 2.98 us
    all_gather x1 -> x0, waiting for transfers between devices: 149 us -> none  [on_device(): lax.all_gather(moving, 'snap', axis=0, tiled=True)]
    pallas_call x0 -> x1, Pallas kernels: none -> 96.5 us  [exchange(): pl.pallas_call(main_kernel, in_specs=[smem, smem, vmem, hbm, hbm], out_sp...]
    reduce_scatter x1 -> x0, waiting for transfers between devices: 70.5 us -> none  [on_device(): return lax.psum_scatter(product, 'space', scatter_dimension=0, tiled=True)]
    all_to_all x1 -> x0, waiting for transfers between devices: 35.2 us -> none  [on_device(): lax.all_to_all(outgoing, 'space', split_axis=1, concat_axis=1, tiled=True)]
    dot_general x1 -> x0, matrix products: 13.2 us -> none  [on_device(): lax.dot_general(lax.all_gather(moving, 'snap', axis=0, tiled=True), weigh...]
    all_to_all x1 -> x0, starting transfers between devices: 9.58 us -> none  [on_device(): lax.all_to_all(outgoing, 'space', split_axis=1, concat_axis=1, tiled=True)]
    gather x7 -> x0, local copies, waits for them, and re-layouts: 5.49 us -> none  [the longest x1 1.96 us: on_device(): jnp.take(blocks, own_order, axis=1)]
    sort x2 -> x0, other arithmetic: 4.05 us -> none  [the longest x1 2.54 us: on_device(): inverse = jnp.argsort(arrived)]
  transfers between devices with their start and end apart: 3 -> 0, of which waited for: 3 -> 0; matrix products, arithmetic and copies ran while one was open for 1% -> 0% of each run, Pallas kernels for 0% -> 0%
where the time goes in v2:
time: 103 us; the launch traced here: 102 us
  Pallas kernels  96.5 us (94%)
  local copies, waits for them, and re-layouts  2.98 us (3%)
  other arithmetic  2.4 us (2%)
    pallas_call x1, Pallas kernels, exchange(): pl.pallas_call(main_kernel, in_specs=[smem, smem, vmem, hbm, hbm], out_sp...  96.5 us

profile of v2, /device:TPU:2, one launch (start us, length us, event | category | flops | bytes accessed | tf_op | source)
XLA Modules:
  0.0 101.9 jit_solution(3140100950865983545)
XLA Ops:
  0.0 0.7 fusion.1
  0.7 0.1 and.49
  0.8 0.7 broadcast_subtract_fusion
  1.5 0.1 sub.23
  1.6 0.1 div.21
  1.7 0.6 convert_reduce_fusion
  2.3 0.2 select_reduce_fusion
  2.5 0.2 select_reduce_fusion.1
  2.7 0.7 copy.5.idx_a
  3.4 0.7 copy.6.idx_p
  4.0 96.5 %exchange.1 = f32[64,128]{1,0:T(8,128)} custom-call(s32[16,6]{1,0:T(8,128)} %copy.5.idx_a, s32[16,6]{1,0:T(8,128)} %copy.6.idx_p, f32[96,1,128]{2,1,0:T(1,128)} %bitcast.5, bf16[64,12288]{1,0:T(8,128)(2,1)} %a_hbm.1, bf16[128,12288]{1,0:T(8,128)(2,1)} %p_hbm.1), custom_call_target="tpu_custom_call" | custom-call | tf_op jit(solution)/shard_map/exchange/pallas_call | solution.py:265
  100.6 1.4 %copy.8 = f32[64,128]{1,0:T(8,128)} copy(f32[64,128]{1,0:T(8,128)} %exchange.1) | data formatting | bytes 65536
  (5 shorter events, 0.1 us)

commit v3 on v2

v3 whole, which is shorter than its diff:
```python
import functools
import jax
import jax.numpy as jnp
from jax import lax
from jax.experimental import pallas as pl
from jax.experimental.pallas import tpu as pltpu
from jax.sharding import PartitionSpec as P

PEN = 128
NX, NZ = 4, 8
TILES = 16
DEV_PEN = 96
SHARE = 6
MESH = pl.DeviceIdType.MESH
BLK = SHARE * PEN
KLOC = 4 * BLK


def where_am_i():
    space = lax.axis_index("space")
    snap = lax.axis_index("snap")
    return space // 2, space % 2, snap // 8, (snap // 2) % NX, snap % 2


def device(z, ylo, yh, x, c):
    return {"space": z * 2 + ylo, "snap": yh * 8 + x * 2 + c}


ORDER = (0, 1, 7, 2, 6, 4, 3, 5)
XORDER = (1, 3, 2)
ROWS = 256
STEPS = 1024 // ROWS


def main_kernel(idx_a, idx_p, w_ref, a_hbm, p_hbm, o_ref, a_v, p_v, asort, psort, r1, afin, pfin,
                own, psend, rx, tot, r2,
                lsem, ss1, rs1, ssp, rsp, ssy, rsy, ssc, rsc, ssx, rsx, ss2, rs2):
    z, ylo, yh, x, c = where_am_i()
    space = z * 2 + ylo

    def remote(src, dst, ss, rs, dev):
        return pltpu.make_async_remote_copy(src_ref=src, dst_ref=dst, send_sem=ss, recv_sem=rs,
                                            device_id=dev, device_id_type=MESH)

    def arrived(ref, sem):
        pltpu.make_async_copy(ref, ref, sem).wait()

    def load(hbm, v, sem):
        def body(i, carry):
            lane = pl.ds(pl.multiple_of(i * PEN, PEN), PEN)
            pltpu.make_async_copy(hbm.at[:, lane], v.at[i], sem).start()
            return carry
        lax.fori_loop(0, DEV_PEN, body, 0)

    load(a_hbm, a_v, lsem.at[0])

    bar = pltpu.get_barrier_semaphore()

    def greet(dev):
        pl.semaphore_signal(bar, inc=1, device_id=dev, device_id_type=MESH)

    for zi in range(2):
        for xs in range(NX):
            dev = device((z - x - 4 * zi + 2 * NZ) % NZ, ylo, yh, xs, c)
            if zi == 0 and xs == 0:
                @pl.when(x != 0)
                def _():
                    greet(dev)
            else:
                greet(dev)
    for d in range(1, NX):
        greet(device(z, ylo, yh, (x + d) % NX, c))
    greet(device(z, ylo, 1 - yh, x, c))
    greet(device(z, 1 - ylo, 0, x, c))
    greet(device(z, 1 - ylo, 1, x, c))
    greet(device(z, ylo, yh, x, 1 - c))
    for d in range(1, TILES):
        to = (space + d) % TILES
        greet(device(to // 2, to % 2, yh, x, c))

    arrived(a_v, lsem.at[0])
    for dz in range(NZ):
        for lt in range(2):
            t = ((z + dz) % NZ) * 2 + lt
            for r in range(SHARE):
                v = a_v[idx_a[r, t]]
                for h in range(2):
                    asort[dz, lt, h, :, r * PEN:(r + 1) * PEN] = v[h * 32:(h + 1) * 32]

    pl.semaphore_wait(bar, 7 + 3 + 3 + 1 + 15 + (x + NX - 1) // NX)

    def a_copy(h, dz, l):
        lt = (1 - ylo + l) % 2
        return remote(asort.at[dz, lt, h], r1.at[dz // NX, x, lt, h], ss1.at[dz, l, h],
                      rs1.at[dz // NX, x, lt, h], device((z + dz) % NZ, ylo, yh, dz % NX, c))

    for h in range(2):
        for dz in ORDER:
            for l in range(2):
                if dz == 0:
                    lt = (1 - ylo + l) % 2

                    @pl.when(x == 0)
                    def _():
                        pltpu.make_async_copy(asort.at[0, lt, h], r1.at[0, 0, lt, h], rs1.at[0, 0, lt, h]).start()

                    @pl.when(x != 0)
                    def _():
                        a_copy(h, 0, l).start()
                else:
                    a_copy(h, dz, l).start()
    load(p_hbm, p_v, lsem.at[1])

    def p_copy(slot):
        d = XORDER[slot - 1]
        return remote(psort.at[d], pfin.at[XORDER.index(NX - d) + 1], ssp.at[slot - 1],
                      rsp.at[XORDER.index(NX - d) + 1], device(z, ylo, yh, (x + d) % NX, c))

    own_p = pltpu.make_async_copy(psort.at[0], pfin.at[0], rsp.at[0])
    arrived(p_v, lsem.at[1])
    for step, d in enumerate(XORDER + (0,)):
        for zi in range(2):
            dz = (x + d) % NX + NX * zi
            for ls in range(2):
                src = ((z - dz + NZ) % NZ) * 2 + ls
                for r in range(SHARE):
                    i = idx_p[r, src]
                    at = ((zi * 2 + ls) * SHARE + r) * PEN
                    psort[d, :, at:at + PEN] = (
                        p_v[i].astype(jnp.float32) * w_ref[i]).astype(jnp.bfloat16)
        if step >= 1:
            p_copy(step).start()
    own_p.start()

    flip = x // 3
    chunks = [(h, j, d, l) for h in range(2) for j in range(2) for d in (0, 1, 3, 2) for l in range(2)]

    def block(h, ys, xs, core, zi, ls):
        lane = pl.ds(pl.multiple_of((zi * 2 + ls) * BLK, BLK), BLK)
        return afin.at[h, ys * 8 + xs * 2 + core, :, lane]

    def y_copies(k):
        h, j, d, l = chunks[k]
        zi, xs, lt = (j + flip) % 2, (x + d) % NX, (1 - ylo + l) % 2
        src = r1.at[zi, xs, lt, h]
        dst = block(h, yh, xs, c, zi, ylo)
        rs = rsy.at[h, yh, xs, zi, ylo]
        out = [remote(src, dst, ssy.at[k, 0], rs, device(z, lt, 1 - yh, x, c))]
        if l == 0:
            out.append(remote(src, dst, ssy.at[k, 1], rs, device(z, lt, yh, x, c)))
        return src, rs1.at[zi, xs, lt, h], out, dst, rs

    def sources(k):
        h, j, d, l = chunks[k]
        zi, xs = (j + flip) % 2, (x + d) % NX
        ls = (ylo + 1 - l) % 2
        return [(h, (yh + dy) % 2, xs, zi, ls, dy) for dy in range(2)]

    def c_copies(k):
        return [remote(block(h, ys, xs, c, zi, ls), block(h, ys, xs, c, zi, ls), ssc.at[k, dy],
                       rsc.at[h, ys, xs, zi, ls], device(z, ylo, yh, x, 1 - c))
                for h, ys, xs, zi, ls, dy in sources(k)]

    lag = 6
    for k in range(len(chunks) + lag):
        if k < len(chunks):
            src, sem, out, dst, rs = y_copies(k)
            arrived(src, sem)
            for cp in out:
                cp.start()
            if chunks[k][3] == 1:
                pltpu.make_async_copy(src, dst, rs).start()
        if k >= lag:
            for (h, ys, xs, zi, ls, _), cp in zip(sources(k - lag), c_copies(k - lag)):
                arrived(block(h, ys, xs, c, zi, ls), rsy.at[h, ys, xs, zi, ls])
                cp.start()
    for k in range(len(chunks)):
        for h, ys, xs, zi, ls, _ in sources(k):
            arrived(block(h, ys, xs, 1 - c, zi, ls), rsc.at[h, ys, xs, zi, ls])

    blocks = ROWS // 32

    def part(i):
        return i // 2, (z // 4 + i % 2) % 2 * blocks

    def lhs(i):
        h, at = part(i)
        return afin[h, pl.ds(at, blocks)].reshape(ROWS, KLOC)

    def times(a, b):
        return lax.dot_general(a, b, (((1,), (1,)), ((), ())), preferred_element_type=jnp.float32)

    def x_copy(slot, i):
        d = XORDER[slot - 1]
        back = XORDER.index(NX - d)
        return remote(psend.at[slot - 1, i], rx.at[back, i], ssx.at[slot - 1, i],
                      rsx.at[back, i], device(z, ylo, yh, (x + d) % NX, c))

    arrived(pfin.at[0], rsp.at[0])
    arrived(pfin.at[1], rsp.at[1])
    for i in range(STEPS):
        v = times(lhs(i), pfin[0:2].reshape(256, KLOC))
        own[i] = v[:, :128]
        psend[0, i] = v[:, 128:].astype(psend.dtype)
        x_copy(1, i).start()
    for slot in (2, 3):
        arrived(pfin.at[slot], rsp.at[slot])
        for i in range(STEPS):
            psend[slot - 1, i] = times(lhs(i), pfin[slot]).astype(psend.dtype)
            x_copy(slot, i).start()

    def f_copy(i, j):
        h, at = part(i)
        to = at + j
        return remote(tot.at[h, to], r2.at[h, space], ss2.at[i, j], rs2.at[h, space],
                      device(to // 2, to % 2, yh, x, c))

    for i in range(STEPS):
        h, at = part(i)
        total = own[i]
        for slot in range(3):
            arrived(rx.at[slot, i], rsx.at[slot, i])
            total = total + rx[slot, i].astype(jnp.float32)
        tot[h, pl.ds(at, blocks)] = total.reshape(blocks, 32, 128)
        for j in range(blocks):
            @pl.when(at + j != space)
            def _():
                f_copy(i, j).start()
    for h in range(2):
        acc = tot[h, space]
        for d in range(1, TILES):
            frm = (space + d) % TILES
            arrived(r2.at[h, frm], rs2.at[h, frm])
            acc = acc + r2[h, frm]
        o_ref[h * 32:(h + 1) * 32] = acc

    for h in range(2):
        for l in range(2):
            @pl.when(x != 0)
            def _():
                a_copy(h, 0, l).wait_send()
            for dz in range(1, NZ):
                a_copy(h, dz, l).wait_send()
    for slot in range(1, NX):
        p_copy(slot).wait_send()
        for i in range(STEPS):
            x_copy(slot, i).wait_send()
    for k in range(len(chunks)):
        for cp in y_copies(k)[2] + c_copies(k):
            cp.wait_send()
    for i in range(STEPS):
        for j in range(blocks):
            @pl.when(part(i)[1] + j != space)
            def _():
                f_copy(i, j).wait_send()


def exchange(idx_a, idx_p, weights, adjoint, primal):
    bf, f32 = jnp.bfloat16, jnp.float32
    dma = pltpu.SemaphoreType.DMA
    smem = pl.BlockSpec(memory_space=pltpu.SMEM)
    hbm = pl.BlockSpec(memory_space=pl.ANY)
    vmem = pl.BlockSpec(memory_space=pltpu.VMEM)
    return pl.pallas_call(
        main_kernel,
        in_specs=[smem, smem, vmem, hbm, hbm],
        out_specs=vmem,
        out_shape=jax.ShapeDtypeStruct((64, 128), f32),
        scratch_shapes=[
            pltpu.VMEM((DEV_PEN, 64, PEN), bf),
            pltpu.VMEM((DEV_PEN, 128, PEN), bf),
            pltpu.VMEM((NZ, 2, 2, 32, BLK), bf),
            pltpu.VMEM((NX, 128, KLOC), bf),
            pltpu.VMEM((2, NX, 2, 2, 32, BLK), bf),
            pltpu.VMEM((2, 16, 32, KLOC), bf),
            pltpu.VMEM((NX, 128, KLOC), bf),
            pltpu.VMEM((STEPS, ROWS, 128), f32),
            pltpu.VMEM((3, STEPS, ROWS, 128), bf),
            pltpu.VMEM((3, STEPS, ROWS, 128), bf),
            pltpu.VMEM((2, TILES, 32, 128), f32),
            pltpu.VMEM((2, TILES, 32, 128), f32),
            dma((2,)),
            dma((NZ, 2, 2)), dma((2, NX, 2, 2)),
            dma((3,)), dma((NX,)),
            dma((32, 2)), dma((2, 2, NX, 2, 2)),
            dma((32, 2)), dma((2, 2, NX, 2, 2)),
            dma((3, STEPS)), dma((3, STEPS)),
            dma((STEPS, ROWS // 32)), dma((2, TILES)),
        ],
        compiler_params=pltpu.CompilerParams(
            collective_id=0, has_side_effects=True, vmem_limit_bytes=60 * 1024 * 1024),
        name="exchange",
    )(idx_a.T, idx_p.T, weights.reshape(DEV_PEN, 1, PEN), adjoint, primal)


def on_device(primal, adjoint_pencils, weights, pencil_map):
    space = lax.axis_index("space")
    maps = pencil_map.reshape(TILES, DEV_PEN)
    target = maps // DEV_PEN
    before = jnp.arange(DEV_PEN)[None, :] < jnp.arange(DEV_PEN)[:, None]
    rank = jnp.sum((target[:, :, None] == target[:, None, :]) & before[None], axis=2, dtype=jnp.int32)
    of_rank = jnp.arange(SHARE, dtype=jnp.int32)[None, :, None]
    here = (target == space)[:, None, :] & (rank[:, None, :] == of_rank)
    idx_p = jnp.sum(jnp.where(here, maps[:, None, :] - space * DEV_PEN, 0), axis=2, dtype=jnp.int32)
    own_target = lax.dynamic_index_in_dim(target, space, 0, keepdims=True)
    own_rank = lax.dynamic_index_in_dim(rank, space, 0, keepdims=True)
    to = (own_target == jnp.arange(TILES, dtype=jnp.int32)[:, None])[:, None, :] & (own_rank[:, None, :] == of_rank)
    idx_a = jnp.sum(jnp.where(to, jnp.arange(DEV_PEN, dtype=jnp.int32), 0), axis=2, dtype=jnp.int32)
    return exchange(idx_a, idx_p, weights, adjoint_pencils, primal)


def solution(mesh):
    placed = (P("snap", "space"), P("snap", "space"), P("space"), P())
    return jax.shard_map(
        on_device, mesh=mesh, in_specs=placed, out_specs=P("space", "snap"), check_vma=False
    )
```

time: 103 us -> 100 us (0.971)
  Pallas kernels: 96.5 us -> 93.3 us
  local copies, waits for them, and re-layouts: 2.98 us -> 1.61 us
  other arithmetic: 2.4 us -> 3.59 us
    pallas_call x1, Pallas kernels: 96.5 us -> 93.3 us  [exchange(): pl.pallas_call(main_kernel, in_specs=[smem, smem, vmem, hbm, hbm], out_sp...]
    reduce_sum x2 -> x0, local copies, waits for them, and re-layouts: 1.36 us -> none  [the longest x1 0.68 us: on_device(): jnp.sum(jnp.where(to, jnp.arange(DEV_PEN, dtype=jnp.int32), 0), axis=2, d...]
where the time goes in v3:
time: 100 us; the launch traced here: 98.5 us
  Pallas kernels  93.3 us (93%)
  other arithmetic  3.59 us (4%)
  local copies, waits for them, and re-layouts  1.61 us (2%)
    pallas_call x1, Pallas kernels, exchange(): pl.pallas_call(main_kernel, in_specs=[smem, smem, vmem, hbm, hbm], out_sp...  93.3 us

profile of v3, /device:TPU:2, one launch (start us, length us, event | category | flops | bytes accessed | tf_op | source)
XLA Modules:
  0.0 98.5 jit_solution(3233127637410245933)
XLA Ops:
  0.0 0.7 fusion.1
  0.7 0.1 and.49
  0.8 0.7 broadcast_subtract_fusion
  1.5 0.1 sub.23
  1.6 0.1 div.21
  1.7 0.6 convert_reduce_fusion
  2.3 0.8 select_reduce_fusion
  3.1 0.8 select_reduce_fusion.1
  3.8 93.3 %exchange.1 = f32[64,128]{1,0:T(8,128)} custom-call(s32[6,16]{1,0:T(8,128)} %bitcast.8, s32[6,16]{1,0:T(8,128)} %bitcast.9, f32[96,1,128]{2,1,0:T(1,128)} %bitcast.7, bf16[64,12288]{1,0:T(8,128)(2,1)} %a_hbm.1, bf16[128,12288]{1,0:T(8,128)(2,1)} %p_hbm.1), custom_call_target="tpu_custom_call" | custom-call | tf_op jit(solution)/shard_map/exchange/pallas_call | solution.py:264
  97.1 1.4 %copy.6 = f32[64,128]{1,0:T(8,128)} copy(f32[64,128]{1,0:T(8,128)} %exchange.1) | data formatting | bytes 65536
  (5 shorter events, 0.0 us)

commit v4 on v3

--- a/solution.py
+++ b/solution.py
@@ -32,8 +32,31 @@
 STEPS = 1024 // ROWS
 
 
-def main_kernel(idx_a, idx_p, w_ref, a_hbm, p_hbm, o_ref, a_v, p_v, asort, psort, r1, afin, pfin,
-                own, psend, rx, tot, r2,
+def sort_kernel(idx_a, a_ref, o_ref):
+    z, _, _, _, _ = where_am_i()
+    for dz in range(NZ):
+        for lt in range(2):
+            t = ((z + dz) % NZ) * 2 + lt
+            for r in range(SHARE):
+                lane = pl.ds(pl.multiple_of(idx_a[r, t] * PEN, PEN), PEN)
+                o_ref[0, dz, lt, :, r * PEN:(r + 1) * PEN] = a_ref[:, lane]
+
+
+def sort_adjoint(idx_a, adjoint):
+    rows, points = adjoint.shape
+    return pl.pallas_call(
+        sort_kernel,
+        grid=(2,),
+        in_specs=[pl.BlockSpec(memory_space=pltpu.SMEM),
+                  pl.BlockSpec((rows // 2, points), lambda h: (h, 0))],
+        out_specs=pl.BlockSpec((1, NZ, 2, rows // 2, BLK), lambda h: (h, 0, 0, 0, 0)),
+        out_shape=jax.ShapeDtypeStruct((2, NZ, 2, rows // 2, BLK), jnp.bfloat16),
+        name="sort_adjoint",
+    )(idx_a, adjoint)
+
+
+def main_kernel(idx_p, w_ref, asort, p_hbm, o_ref, p_v, psort, r1, afin, pfin,
+                own, psend, rx, tot, fsend, r2,
                 lsem, ss1, rs1, ssp, rsp, ssy, rsy, ssc, rsc, ssx, rsx, ss2, rs2):
     z, ylo, yh, x, c = where_am_i()
     space = z * 2 + ylo
@@ -52,7 +75,6 @@
             return carry
         lax.fori_loop(0, DEV_PEN, body, 0)
 
-    load(a_hbm, a_v, lsem.at[0])
 
     bar = pltpu.get_barrier_semaphore()
 
@@ -78,47 +100,12 @@
         to = (space + d) % TILES
         greet(device(to // 2, to % 2, yh, x, c))
 
-    arrived(a_v, lsem.at[0])
-    for dz in range(NZ):
-        for lt in range(2):
-            t = ((z + dz) % NZ) * 2 + lt
-            for r in range(SHARE):
-                v = a_v[idx_a[r, t]]
-                for h in range(2):
-                    asort[dz, lt, h, :, r * PEN:(r + 1) * PEN] = v[h * 32:(h + 1) * 32]
-
-    pl.semaphore_wait(bar, 7 + 3 + 3 + 1 + 15 + (x + NX - 1) // NX)
-
-    def a_copy(h, dz, l):
-        lt = (1 - ylo + l) % 2
-        return remote(asort.at[dz, lt, h], r1.at[dz // NX, x, lt, h], ss1.at[dz, l, h],
-                      rs1.at[dz // NX, x, lt, h], device((z + dz) % NZ, ylo, yh, dz % NX, c))
-
-    for h in range(2):
-        for dz in ORDER:
-            for l in range(2):
-                if dz == 0:
-                    lt = (1 - ylo + l) % 2
-
-                    @pl.when(x == 0)
-                    def _():
-                        pltpu.make_async_copy(asort.at[0, lt, h], r1.at[0, 0, lt, h], rs1.at[0, 0, lt, h]).start()
-
-                    @pl.when(x != 0)
-                    def _():
-                        a_copy(h, 0, l).start()
-                else:
-                    a_copy(h, dz, l).start()
-    load(p_hbm, p_v, lsem.at[1])
-
     def p_copy(slot):
         d = XORDER[slot - 1]
         return remote(psort.at[d], pfin.at[XORDER.index(NX - d) + 1], ssp.at[slot - 1],
                       rsp.at[XORDER.index(NX - d) + 1], device(z, ylo, yh, (x + d) % NX, c))
 
-    own_p = pltpu.make_async_copy(psort.at[0], pfin.at[0], rsp.at[0])
-    arrived(p_v, lsem.at[1])
-    for step, d in enumerate(XORDER + (0,)):
+    def sort_p(d):
         for zi in range(2):
             dz = (x + d) % NX + NX * zi
             for ls in range(2):
@@ -128,8 +115,41 @@
                     at = ((zi * 2 + ls) * SHARE + r) * PEN
                     psort[d, :, at:at + PEN] = (
                         p_v[i].astype(jnp.float32) * w_ref[i]).astype(jnp.bfloat16)
-        if step >= 1:
-            p_copy(step).start()
+
+    own_p = pltpu.make_async_copy(psort.at[0], pfin.at[0], rsp.at[0])
+    load(p_hbm, p_v, lsem.at[0])
+    arrived(p_v, lsem.at[0])
+    sort_p(XORDER[0])
+
+    pl.semaphore_wait(bar, 7 + 3 + 3 + 1 + 15 + (x + NX - 1) // NX)
+
+    def a_copy(h, dz, l):
+        lt = (1 - ylo + l) % 2
+        return remote(asort.at[h, dz, lt], r1.at[dz // NX, x, lt, h], ss1.at[dz, l, h],
+                      rs1.at[dz // NX, x, lt, h], device((z + dz) % NZ, ylo, yh, dz % NX, c))
+
+    p_copy(1).start()
+    for h in range(2):
+        for dz in ORDER:
+            for l in range(2):
+                if dz == 0:
+                    lt = (1 - ylo + l) % 2
+
+                    @pl.when(x == 0)
+                    def _():
+                        pltpu.make_async_copy(asort.at[h, 0, lt], r1.at[0, 0, lt, h], rs1.at[0, 0, lt, h]).start()
+
+                    @pl.when(x != 0)
+                    def _():
+                        a_copy(h, 0, l).start()
+                else:
+                    a_copy(h, dz, l).start()
+
+    sort_p(XORDER[1])
+    sort_p(XORDER[2])
+    p_copy(2).start()
+    sort_p(0)
+    p_copy(3).start()
     own_p.start()
 
     flip = x // 3
@@ -212,7 +232,7 @@
     def f_copy(i, j):
         h, at = part(i)
         to = at + j
-        return remote(tot.at[h, to], r2.at[h, space], ss2.at[i, j], rs2.at[h, space],
+        return remote(fsend.at[h, to], r2.at[h, space], ss2.at[i, j], rs2.at[h, space],
                       device(to // 2, to % 2, yh, x, c))
 
     for i in range(STEPS):
@@ -221,7 +241,9 @@
         for slot in range(3):
             arrived(rx.at[slot, i], rsx.at[slot, i])
             total = total + rx[slot, i].astype(jnp.float32)
-        tot[h, pl.ds(at, blocks)] = total.reshape(blocks, 32, 128)
+        total = total.reshape(blocks, 32, 128)
+        fsend[h, pl.ds(at, blocks)] = total.astype(fsend.dtype)
+        tot[h, pl.ds(at, blocks)] = total
         for j in range(blocks):
             @pl.when(at + j != space)
             def _():
@@ -231,7 +253,7 @@
         for d in range(1, TILES):
             frm = (space + d) % TILES
             arrived(r2.at[h, frm], rs2.at[h, frm])
-            acc = acc + r2[h, frm]
+            acc = acc + r2[h, frm].astype(jnp.float32)
         o_ref[h * 32:(h + 1) * 32] = acc
 
     for h in range(2):
@@ -255,7 +277,7 @@
                 f_copy(i, j).wait_send()
 
 
-def exchange(idx_a, idx_p, weights, adjoint, primal):
+def exchange(idx_p, weights, a_sorted, primal):
     bf, f32 = jnp.bfloat16, jnp.float32
     dma = pltpu.SemaphoreType.DMA
     smem = pl.BlockSpec(memory_space=pltpu.SMEM)
@@ -263,13 +285,11 @@
     vmem = pl.BlockSpec(memory_space=pltpu.VMEM)
     return pl.pallas_call(
         main_kernel,
-        in_specs=[smem, smem, vmem, hbm, hbm],
+        in_specs=[smem, vmem, hbm, hbm],
         out_specs=vmem,
         out_shape=jax.ShapeDtypeStruct((64, 128), f32),
         scratch_shapes=[
-            pltpu.VMEM((DEV_PEN, 64, PEN), bf),
             pltpu.VMEM((DEV_PEN, 128, PEN), bf),
-            pltpu.VMEM((NZ, 2, 2, 32, BLK), bf),
             pltpu.VMEM((NX, 128, KLOC), bf),
             pltpu.VMEM((2, NX, 2, 2, 32, BLK), bf),
             pltpu.VMEM((2, 16, 32, KLOC), bf),
@@ -278,8 +298,9 @@
             pltpu.VMEM((3, STEPS, ROWS, 128), bf),
             pltpu.VMEM((3, STEPS, ROWS, 128), bf),
             pltpu.VMEM((2, TILES, 32, 128), f32),
-            pltpu.VMEM((2, TILES, 32, 128), f32),
-            dma((2,)),
+            pltpu.VMEM((2, TILES, 32, 128), bf),
+            pltpu.VMEM((2, TILES, 32, 128), bf),
+            dma((1,)),
             dma((NZ, 2, 2)), dma((2, NX, 2, 2)),
             dma((3,)), dma((NX,)),
             dma((32, 2)), dma((2, 2, NX, 2, 2)),
@@ -290,7 +311,7 @@
         compiler_params=pltpu.CompilerParams(
             collective_id=0, has_side_effects=True, vmem_limit_bytes=60 * 1024 * 1024),
         name="exchange",
-    )(idx_a.T, idx_p.T, weights.reshape(DEV_PEN, 1, PEN), adjoint, primal)
+    )(idx_p.T, weights.reshape(DEV_PEN, 1, PEN), a_sorted, primal)
 
 
 def on_device(primal, adjoint_pencils, weights, pencil_map):
@@ -306,7 +327,7 @@
     own_rank = lax.dynamic_index_in_dim(rank, space, 0, keepdims=True)
     to = (own_target == jnp.arange(TILES, dtype=jnp.int32)[:, None])[:, None, :] & (own_rank[:, None, :] == of_rank)
     idx_a = jnp.sum(jnp.where(to, jnp.arange(DEV_PEN, dtype=jnp.int32), 0), axis=2, dtype=jnp.int32)
-    return exchange(idx_a, idx_p, weights, adjoint_pencils, primal)
+    return exchange(idx_p, weights, sort_adjoint(idx_a.T, adjoint_pencils), primal)
 
 
 def solution(mesh):

time: 100 us -> 106 us (1.060)
  the two profiles are of different devices: /device:TPU:2 before, /device:TPU:1 now
where the time goes in v4:
time: 106 us; the launch traced here: 105 us
  Pallas kernels  100 us (94%)
  other arithmetic  3.58 us (3%)
  local copies, waits for them, and re-layouts  1.62 us (2%)
    pallas_call x1, Pallas kernels, exchange(): pl.pallas_call(main_kernel, in_specs=[smem, vmem, hbm, hbm], out_specs=vm...  97.4 us
    pallas_call x1, Pallas kernels, sort_adjoint(): pl.pallas_call(sort_kernel, grid=(2,), in_specs=[pl.BlockSpec(memory_spac...  2.55 us

profile of v4, /device:TPU:1, one launch (start us, length us, event | category | flops | bytes accessed | tf_op | source)
XLA Modules:
  0.0 105.2 jit_solution(1681363031999414381)
XLA Ops:
  0.0 0.7 fusion.1
  0.7 0.1 and.49
  0.8 0.7 broadcast_divide_fusion
  1.5 0.1 div.21
  1.6 0.6 convert_reduce_fusion
  2.2 0.8 select_reduce_fusion
  3.0 0.1 sub.23
  3.1 0.8 select_reduce_fusion.1
  3.9 2.6 %sort_adjoint.1.asort = bf16[2,8,2,32,768]{4,3,2,1,0:T(8,128)(2,1)} custom-call(s32[6,16]{1,0:T(8,128)} %bitcast.8, bf16[64,12288]{1,0:T(8,128)(2,1)} %a_ref.1), custom_call_target="tpu_custom_call" | custom-call | tf_op jit(solution)/shard_map/sort_adjoint/pallas_call | solution.py:47
  6.4 97.4 %exchange.1 = f32[64,128]{1,0:T(8,128)} custom-call(s32[6,16]{1,0:T(8,128)} %bitcast.9, f32[96,1,128]{2,1,0:T(1,128)} %bitcast.7, bf16[2,8,2,32,768]{4,3,2,1,0:T(8,128)(2,1)} %sort_adjoint.1.asort, bf16[128,12288]{1,0:T(8,128)(2,1)} %p_hbm.1), custom_call_target="tpu_custom_call" | custom-call | tf_op jit(solution)/shard_map/exchange/pallas_call | solution.py:286
  103.9 1.4 %copy.6 = f32[64,128]{1,0:T(8,128)} copy(f32[64,128]{1,0:T(8,128)} %exchange.1) | data formatting | bytes 65536
  (5 shorter events, 0.1 us)

commit v5 on v3

--- a/solution.py
+++ b/solution.py
@@ -32,7 +32,7 @@
 STEPS = 1024 // ROWS
 
 
-def main_kernel(idx_a, idx_p, w_ref, a_hbm, p_hbm, o_ref, a_v, p_v, asort, psort, r1, afin, pfin,
+def main_kernel(idx_a, idx_p, w_ref, a_hbm, p_hbm, o_ref, a_v, p_v, a3, p3, asort, psort, r1, afin, pfin,
                 own, psend, rx, tot, r2,
                 lsem, ss1, rs1, ssp, rsp, ssy, rsy, ssc, rsc, ssx, rsx, ss2, rs2):
     z, ylo, yh, x, c = where_am_i()
@@ -45,14 +45,10 @@
     def arrived(ref, sem):
         pltpu.make_async_copy(ref, ref, sem).wait()
 
-    def load(hbm, v, sem):
-        def body(i, carry):
-            lane = pl.ds(pl.multiple_of(i * PEN, PEN), PEN)
-            pltpu.make_async_copy(hbm.at[:, lane], v.at[i], sem).start()
-            return carry
-        lax.fori_loop(0, DEV_PEN, body, 0)
-
-    load(a_hbm, a_v, lsem.at[0])
+    load_a = pltpu.make_async_copy(a_hbm, a_v, lsem.at[0])
+    load_p = pltpu.make_async_copy(p_hbm, p_v, lsem.at[1])
+    load_a.start()
+    load_p.start()
 
     bar = pltpu.get_barrier_semaphore()
 
@@ -78,14 +74,21 @@
         to = (space + d) % TILES
         greet(device(to // 2, to % 2, yh, x, c))
 
-    arrived(a_v, lsem.at[0])
+    load_a.wait()
+    for i in range(DEV_PEN):
+        a3[i] = a_v[:, i * PEN:(i + 1) * PEN]
     for dz in range(NZ):
         for lt in range(2):
             t = ((z + dz) % NZ) * 2 + lt
             for r in range(SHARE):
-                v = a_v[idx_a[r, t]]
+                v = a3[idx_a[r, t]]
                 for h in range(2):
                     asort[dz, lt, h, :, r * PEN:(r + 1) * PEN] = v[h * 32:(h + 1) * 32]
+
+    load_p.wait()
+    for i in range(DEV_PEN):
+        span = slice(i * PEN, (i + 1) * PEN)
+        p3[i] = (p_v[:, span].astype(jnp.float32) * w_ref[:, span]).astype(jnp.bfloat16)
 
     pl.semaphore_wait(bar, 7 + 3 + 3 + 1 + 15 + (x + NX - 1) // NX)
 
@@ -109,7 +112,6 @@
                         a_copy(h, 0, l).start()
                 else:
                     a_copy(h, dz, l).start()
-    load(p_hbm, p_v, lsem.at[1])
 
     def p_copy(slot):
         d = XORDER[slot - 1]
@@ -117,7 +119,6 @@
                       rsp.at[XORDER.index(NX - d) + 1], device(z, ylo, yh, (x + d) % NX, c))
 
     own_p = pltpu.make_async_copy(psort.at[0], pfin.at[0], rsp.at[0])
-    arrived(p_v, lsem.at[1])
     for step, d in enumerate(XORDER + (0,)):
         for zi in range(2):
             dz = (x + d) % NX + NX * zi
@@ -126,8 +127,7 @@
                 for r in range(SHARE):
                     i = idx_p[r, src]
                     at = ((zi * 2 + ls) * SHARE + r) * PEN
-                    psort[d, :, at:at + PEN] = (
-                        p_v[i].astype(jnp.float32) * w_ref[i]).astype(jnp.bfloat16)
+                    psort[d, :, at:at + PEN] = p3[i]
         if step >= 1:
             p_copy(step).start()
     own_p.start()
@@ -267,6 +267,8 @@
         out_specs=vmem,
         out_shape=jax.ShapeDtypeStruct((64, 128), f32),
         scratch_shapes=[
+            pltpu.VMEM(adjoint.shape, bf),
+            pltpu.VMEM(primal.shape, bf),
             pltpu.VMEM((DEV_PEN, 64, PEN), bf),
             pltpu.VMEM((DEV_PEN, 128, PEN), bf),
             pltpu.VMEM((NZ, 2, 2, 32, BLK), bf),
@@ -290,7 +292,7 @@
         compiler_params=pltpu.CompilerParams(
             collective_id=0, has_side_effects=True, vmem_limit_bytes=60 * 1024 * 1024),
         name="exchange",
-    )(idx_a.T, idx_p.T, weights.reshape(DEV_PEN, 1, PEN), adjoint, primal)
+    )(idx_a.T, idx_p.T, weights[None], adjoint, primal)
 
 
 def on_device(primal, adjoint_pencils, weights, pencil_map):

time: 100 us -> 97.9 us (0.979)
  Pallas kernels: 93.3 us -> 92.1 us
    pallas_call x1, Pallas kernels: 93.3 us -> 92.1 us  [exchange(): pl.pallas_call(main_kernel, in_specs=[smem, smem, vmem, hbm, hbm], out_sp...]
where the time goes in v5:
time: 97.9 us; the launch traced here: 97.3 us
  Pallas kernels  92.1 us (94%)
  other arithmetic  3.59 us (4%)
  local copies, waits for them, and re-layouts  1.61 us (2%)
    pallas_call x1, Pallas kernels, exchange(): pl.pallas_call(main_kernel, in_specs=[smem, smem, vmem, hbm, hbm], out_sp...  92.1 us

profile of v5, /device:TPU:2, one launch (start us, length us, event | category | flops | bytes accessed | tf_op | source)
XLA Modules:
  0.0 97.3 jit_solution(1791283785269637780)
XLA Ops:
  0.0 0.7 fusion.1
  0.7 0.1 and.49
  0.8 0.7 broadcast_subtract_fusion
  1.5 0.1 sub.23
  1.6 0.1 div.21
  1.7 0.6 convert_reduce_fusion
  2.3 0.8 select_reduce_fusion
  3.1 0.8 select_reduce_fusion.1
  3.8 92.1 %exchange.1 = f32[64,128]{1,0:T(8,128)} custom-call(s32[6,16]{1,0:T(8,128)} %bitcast.8, s32[6,16]{1,0:T(8,128)} %bitcast.9, f32[1,12288]{1,0:T(1,128)} %bitcast.7, bf16[64,12288]{1,0:T(8,128)(2,1)} %a_hbm.1, bf16[128,12288]{1,0:T(8,128)(2,1)} %p_hbm.1), custom_call_target="tpu_custom_call" | custom-call | tf_op jit(solution)/shard_map/exchange/pallas_call | solution.py:264
  95.9 1.4 %copy.6 = f32[64,128]{1,0:T(8,128)} copy(f32[64,128]{1,0:T(8,128)} %exchange.1) | data formatting | bytes 65536
  (5 shorter events, 0.0 us)

commit v6 on v5

--- a/solution.py
+++ b/solution.py
@@ -29,14 +29,12 @@
 ORDER = (0, 1, 7, 2, 6, 4, 3, 5)
 XORDER = (1, 3, 2)
 ROWS = 256
-STEPS = 1024 // ROWS
 
 
 def main_kernel(idx_a, idx_p, w_ref, a_hbm, p_hbm, o_ref, a_v, p_v, a3, p3, asort, psort, r1, afin, pfin,
-                own, psend, rx, tot, r2,
-                lsem, ss1, rs1, ssp, rsp, ssy, rsy, ssc, rsc, ssx, rsx, ss2, rs2):
+                keep, ysend, yrecv, zsum, zsend, zrecv, xsend, xrecv,
+                lsem, ss1, rs1, ssp, rsp, ssy, rsy, ssc, rsc, ssf, rsf, ssz, rsz, ssx, rsx):
     z, ylo, yh, x, c = where_am_i()
-    space = z * 2 + ylo
 
     def remote(src, dst, ss, rs, dev):
         return pltpu.make_async_remote_copy(src_ref=src, dst_ref=dst, send_sem=ss, recv_sem=rs,
@@ -70,9 +68,8 @@
     greet(device(z, 1 - ylo, 0, x, c))
     greet(device(z, 1 - ylo, 1, x, c))
     greet(device(z, ylo, yh, x, 1 - c))
-    for d in range(1, TILES):
-        to = (space + d) % TILES
-        greet(device(to // 2, to % 2, yh, x, c))
+    for d in range(1, NZ):
+        greet(device((z + d) % NZ, ylo, yh, x, c))
 
     load_a.wait()
     for i in range(DEV_PEN):
@@ -90,7 +87,7 @@
         span = slice(i * PEN, (i + 1) * PEN)
         p3[i] = (p_v[:, span].astype(jnp.float32) * w_ref[:, span]).astype(jnp.bfloat16)
 
-    pl.semaphore_wait(bar, 7 + 3 + 3 + 1 + 15 + (x + NX - 1) // NX)
+    pl.semaphore_wait(bar, 7 + 3 + 3 + 1 + 7 + (x + NX - 1) // NX)
 
     def a_copy(h, dz, l):
         lt = (1 - ylo + l) % 2
@@ -137,7 +134,7 @@
 
     def block(h, ys, xs, core, zi, ls):
         lane = pl.ds(pl.multiple_of((zi * 2 + ls) * BLK, BLK), BLK)
-        return afin.at[h, ys * 8 + xs * 2 + core, :, lane]
+        return afin.at[h, core * NZ + ys * NX + xs, :, lane]
 
     def y_copies(k):
         h, j, d, l = chunks[k]
@@ -178,61 +175,84 @@
         for h, ys, xs, zi, ls, _ in sources(k):
             arrived(block(h, ys, xs, 1 - c, zi, ls), rsc.at[h, ys, xs, zi, ls])
 
-    blocks = ROWS // 32
-
-    def part(i):
-        return i // 2, (z // 4 + i % 2) % 2 * blocks
-
-    def lhs(i):
-        h, at = part(i)
-        return afin[h, pl.ds(at, blocks)].reshape(ROWS, KLOC)
+    def lhs(h, l):
+        at = pl.multiple_of((ylo + 1 - l) % 2 * NZ, NZ)
+        return afin[h, pl.ds(at, NZ)].reshape(ROWS, KLOC)
 
     def times(a, b):
         return lax.dot_general(a, b, (((1,), (1,)), ((), ())), preferred_element_type=jnp.float32)
 
-    def x_copy(slot, i):
+    def over_y(slot, h):
+        return remote(ysend.at[slot, h], yrecv.at[slot, h], ssf.at[slot, h], rsf.at[slot, h],
+                      device(z, 1 - ylo, yh, x, c))
+
+    def over_z(slot, d):
+        to = (z + d) % NZ
+        return remote(zsend.at[slot, to], zrecv.at[slot, z], ssz.at[slot, d - 1], rsz.at[slot, z],
+                      device(to, ylo, yh, x, c))
+
+    def over_x(slot):
         d = XORDER[slot - 1]
         back = XORDER.index(NX - d)
-        return remote(psend.at[slot - 1, i], rx.at[back, i], ssx.at[slot - 1, i],
-                      rsx.at[back, i], device(z, ylo, yh, (x + d) % NX, c))
+        return remote(xsend.at[slot - 1], xrecv.at[back], ssx.at[slot - 1], rsx.at[back],
+                      device(z, ylo, yh, (x + d) % NX, c))
+
+    def to_z(slot):
+        for h in range(2):
+            arrived(yrecv.at[slot, h], rsf.at[slot, h])
+            v = (keep[slot, h] + yrecv[slot, h].astype(jnp.float32)).reshape(NZ, 32, 128)
+            zsum[slot, :, h] = v
+            zsend[slot, :, h] = v.astype(zsend.dtype)
+        for d in (4, 3, 5, 2, 6, 1, 7):
+            over_z(slot, d).start()
+
+    def summed(slot):
+        acc = zsum[slot, z]
+        for d in (1, 7, 2, 6, 3, 5, 4):
+            frm = (z + d) % NZ
+            arrived(zrecv.at[slot, frm], rsz.at[slot, frm])
+            acc = acc + zrecv[slot, frm].astype(jnp.float32)
+        return acc
 
     arrived(pfin.at[0], rsp.at[0])
     arrived(pfin.at[1], rsp.at[1])
-    for i in range(STEPS):
-        v = times(lhs(i), pfin[0:2].reshape(256, KLOC))
-        own[i] = v[:, :128]
-        psend[0, i] = v[:, 128:].astype(psend.dtype)
-        x_copy(1, i).start()
-    for slot in (2, 3):
+    for l in range(2):
+        for h in range(2):
+            v = times(lhs(h, l), pfin[0:2].reshape(256, KLOC))
+            for slot in range(2):
+                w = v[:, slot * 128:(slot + 1) * 128]
+                if l == 0:
+                    ysend[slot, h] = w.astype(ysend.dtype)
+                    over_y(slot, h).start()
+                else:
+                    keep[slot, h] = w
+
+    def one(slot):
         arrived(pfin.at[slot], rsp.at[slot])
-        for i in range(STEPS):
-            psend[slot - 1, i] = times(lhs(i), pfin[slot]).astype(psend.dtype)
-            x_copy(slot, i).start()
-
-    def f_copy(i, j):
-        h, at = part(i)
-        to = at + j
-        return remote(tot.at[h, to], r2.at[h, space], ss2.at[i, j], rs2.at[h, space],
-                      device(to // 2, to % 2, yh, x, c))
-
-    for i in range(STEPS):
-        h, at = part(i)
-        total = own[i]
-        for slot in range(3):
-            arrived(rx.at[slot, i], rsx.at[slot, i])
-            total = total + rx[slot, i].astype(jnp.float32)
-        tot[h, pl.ds(at, blocks)] = total.reshape(blocks, 32, 128)
-        for j in range(blocks):
-            @pl.when(at + j != space)
-            def _():
-                f_copy(i, j).start()
-    for h in range(2):
-        acc = tot[h, space]
-        for d in range(1, TILES):
-            frm = (space + d) % TILES
-            arrived(r2.at[h, frm], rs2.at[h, frm])
-            acc = acc + r2[h, frm]
-        o_ref[h * 32:(h + 1) * 32] = acc
+        for l in range(2):
+            for h in range(2):
+                w = times(lhs(h, l), pfin[slot])
+                if l == 0:
+                    ysend[slot, h] = w.astype(ysend.dtype)
+                    over_y(slot, h).start()
+                else:
+                    keep[slot, h] = w
+
+    one(2)
+    for slot in (1, 0, 2):
+        to_z(slot)
+    one(3)
+    to_z(3)
+    for slot in (1, 2):
+        xsend[slot - 1] = summed(slot)
+        over_x(slot).start()
+    acc = summed(0)
+    xsend[2] = summed(3)
+    over_x(3).start()
+    for slot in range(3):
+        arrived(xrecv.at[slot], rsx.at[slot])
+        acc = acc + xrecv[slot]
+    o_ref[...] = acc.reshape(64, 128)
 
     for h in range(2):
         for l in range(2):
@@ -243,16 +263,15 @@
                 a_copy(h, dz, l).wait_send()
     for slot in range(1, NX):
         p_copy(slot).wait_send()
-        for i in range(STEPS):
-            x_copy(slot, i).wait_send()
+        over_x(slot).wait_send()
     for k in range(len(chunks)):
         for cp in y_copies(k)[2] + c_copies(k):
             cp.wait_send()
-    for i in range(STEPS):
-        for j in range(blocks):
-            @pl.when(part(i)[1] + j != space)
-            def _():
-                f_copy(i, j).wait_send()
+    for slot in range(NX):
+        for h in range(2):
+            over_y(slot, h).wait_send()
+        for d in range(1, NZ):
+            over_z(slot, d).wait_send()
 
 
 def exchange(idx_a, idx_p, weights, adjoint, primal):
@@ -276,18 +295,22 @@
             pltpu.VMEM((2, NX, 2, 2, 32, BLK), bf),
             pltpu.VMEM((2, 16, 32, KLOC), bf),
             pltpu.VMEM((NX, 128, KLOC), bf),
-            pltpu.VMEM((STEPS, ROWS, 128), f32),
-            pltpu.VMEM((3, STEPS, ROWS, 128), bf),
-            pltpu.VMEM((3, STEPS, ROWS, 128), bf),
-            pltpu.VMEM((2, TILES, 32, 128), f32),
-            pltpu.VMEM((2, TILES, 32, 128), f32),
+            pltpu.VMEM((NX, 2, ROWS, 128), f32),
+            pltpu.VMEM((NX, 2, ROWS, 128), bf),
+            pltpu.VMEM((NX, 2, ROWS, 128), bf),
+            pltpu.VMEM((NX, NZ, 2, 32, 128), f32),
+            pltpu.VMEM((NX, NZ, 2, 32, 128), bf),
+            pltpu.VMEM((NX, NZ, 2, 32, 128), bf),
+            pltpu.VMEM((3, 2, 32, 128), f32),
+            pltpu.VMEM((3, 2, 32, 128), f32),
             dma((2,)),
             dma((NZ, 2, 2)), dma((2, NX, 2, 2)),
             dma((3,)), dma((NX,)),
             dma((32, 2)), dma((2, 2, NX, 2, 2)),
             dma((32, 2)), dma((2, 2, NX, 2, 2)),
-            dma((3, STEPS)), dma((3, STEPS)),
-            dma((STEPS, ROWS // 32)), dma((2, TILES)),
+            dma((NX, 2)), dma((NX, 2)),
+            dma((NX, NZ - 1)), dma((NX, NZ)),
+            dma((3,)), dma((3,)),
         ],
         compiler_params=pltpu.CompilerParams(
             collective_id=0, has_side_effects=True, vmem_limit_bytes=60 * 1024 * 1024),

time: 97.9 us -> 96.5 us (0.986)
  Pallas kernels: 92.1 us -> 91 us
    pallas_call x1, Pallas kernels: 92.1 us -> 91 us  [exchange(): pl.pallas_call(main_kernel, in_specs=[smem, smem, vmem, hbm, hbm], out_sp...]
where the time goes in v6:
time: 96.5 us; the launch traced here: 96.2 us
  Pallas kernels  91 us (94%)
  other arithmetic  3.59 us (4%)
  local copies, waits for them, and re-layouts  1.61 us (2%)
    pallas_call x1, Pallas kernels, exchange(): pl.pallas_call(main_kernel, in_specs=[smem, smem, vmem, hbm, hbm], out_sp...  91 us

profile of v6, /device:TPU:2, one launch (start us, length us, event | category | flops | bytes accessed | tf_op | source)
XLA Modules:
  0.0 96.2 jit_solution(5491172525754350794)
XLA Ops:
  0.0 0.7 fusion.1
  0.7 0.1 and.49
  0.8 0.7 broadcast_subtract_fusion
  1.5 0.1 sub.23
  1.6 0.1 div.21
  1.7 0.6 convert_reduce_fusion
  2.3 0.8 select_reduce_fusion
  3.1 0.8 select_reduce_fusion.1
  3.8 91.0 %exchange.1 = f32[64,128]{1,0:T(8,128)} custom-call(s32[6,16]{1,0:T(8,128)} %bitcast.8, s32[6,16]{1,0:T(8,128)} %bitcast.9, f32[1,12288]{1,0:T(1,128)} %bitcast.7, bf16[64,12288]{1,0:T(8,128)(2,1)} %a_hbm.1, bf16[128,12288]{1,0:T(8,128)(2,1)} %p_hbm.1), custom_call_target="tpu_custom_call" | custom-call | tf_op jit(solution)/shard_map/exchange/pallas_call | solution.py:283
  94.8 1.4 %copy.6 = f32[64,128]{1,0:T(8,128)} copy(f32[64,128]{1,0:T(8,128)} %exchange.1) | data formatting | bytes 65536
  (5 shorter events, 0.0 us)

commit v7 on v6

--- a/solution.py
+++ b/solution.py
@@ -158,6 +158,41 @@
                        rsc.at[h, ys, xs, zi, ls], device(z, ylo, yh, x, 1 - c))
                 for h, ys, xs, zi, ls, dy in sources(k)]
 
+    def lhs(h, l):
+        at = pl.multiple_of((ylo + 1 - l) % 2 * NZ, NZ)
+        return afin[h, pl.ds(at, NZ)].reshape(ROWS, KLOC)
+
+    def times(a, b):
+        return lax.dot_general(a, b, (((1,), (1,)), ((), ())), preferred_element_type=jnp.float32)
+
+    def over_y(slot, h):
+        return remote(ysend.at[slot, h], yrecv.at[slot, h], ssf.at[slot, h], rsf.at[slot, h],
+                      device(z, 1 - ylo, yh, x, c))
+
+    def give(slot, h, l, w):
+        if l == 0:
+            ysend[slot, h] = w.astype(ysend.dtype)
+            over_y(slot, h).start()
+        else:
+            keep[slot, h] = w
+
+    def single(slot, h, l):
+        give(slot, h, l, times(lhs(h, l), pfin[slot]))
+
+    def pair(h):
+        for l in range(2):
+            v = times(lhs(h, l), pfin[0:2].reshape(256, KLOC))
+            for slot in range(2):
+                give(slot, h, l, v[:, slot * 128:(slot + 1) * 128])
+
+    def one(slot, h):
+        for l in range(2):
+            single(slot, h, l)
+
+    def from_core(k):
+        for h, ys, xs, zi, ls, _ in sources(k):
+            arrived(block(h, ys, xs, 1 - c, zi, ls), rsc.at[h, ys, xs, zi, ls])
+
     lag = 6
     for k in range(len(chunks) + lag):
         if k < len(chunks):
@@ -171,20 +206,15 @@
             for (h, ys, xs, zi, ls, _), cp in zip(sources(k - lag), c_copies(k - lag)):
                 arrived(block(h, ys, xs, c, zi, ls), rsy.at[h, ys, xs, zi, ls])
                 cp.start()
-    for k in range(len(chunks)):
-        for h, ys, xs, zi, ls, _ in sources(k):
-            arrived(block(h, ys, xs, 1 - c, zi, ls), rsc.at[h, ys, xs, zi, ls])
-
-    def lhs(h, l):
-        at = pl.multiple_of((ylo + 1 - l) % 2 * NZ, NZ)
-        return afin[h, pl.ds(at, NZ)].reshape(ROWS, KLOC)
-
-    def times(a, b):
-        return lax.dot_general(a, b, (((1,), (1,)), ((), ())), preferred_element_type=jnp.float32)
-
-    def over_y(slot, h):
-        return remote(ysend.at[slot, h], yrecv.at[slot, h], ssf.at[slot, h], rsf.at[slot, h],
-                      device(z, 1 - ylo, yh, x, c))
+        if k == 27:
+            for m in range(len(chunks) // 2):
+                from_core(m)
+            arrived(pfin.at[0], rsp.at[0])
+            arrived(pfin.at[1], rsp.at[1])
+            pair(0)
+        if k == 31:
+            arrived(pfin.at[2], rsp.at[2])
+            one(2, 0)
 
     def over_z(slot, d):
         to = (z + d) % NZ
@@ -214,35 +244,18 @@
             acc = acc + zrecv[slot, frm].astype(jnp.float32)
         return acc
 
-    arrived(pfin.at[0], rsp.at[0])
-    arrived(pfin.at[1], rsp.at[1])
+    for k in range(len(chunks) // 2, len(chunks)):
+        from_core(k)
+    pair(1)
+    one(2, 1)
+    for slot in (1, 0):
+        to_z(slot)
+    arrived(pfin.at[3], rsp.at[3])
     for l in range(2):
         for h in range(2):
-            v = times(lhs(h, l), pfin[0:2].reshape(256, KLOC))
-            for slot in range(2):
-                w = v[:, slot * 128:(slot + 1) * 128]
-                if l == 0:
-                    ysend[slot, h] = w.astype(ysend.dtype)
-                    over_y(slot, h).start()
-                else:
-                    keep[slot, h] = w
-
-    def one(slot):
-        arrived(pfin.at[slot], rsp.at[slot])
-        for l in range(2):
-            for h in range(2):
-                w = times(lhs(h, l), pfin[slot])
-                if l == 0:
-                    ysend[slot, h] = w.astype(ysend.dtype)
-                    over_y(slot, h).start()
-                else:
-                    keep[slot, h] = w
-
-    one(2)
-    for slot in (1, 0, 2):
+            single(3, h, l)
+    for slot in (2, 3):
         to_z(slot)
-    one(3)
-    to_z(3)
     for slot in (1, 2):
         xsend[slot - 1] = summed(slot)
         over_x(slot).start()

time: 96.5 us -> 105 us (1.088)
  Pallas kernels: 91 us -> 99.9 us
    pallas_call x1, Pallas kernels: 91 us -> 99.9 us  [exchange(): pl.pallas_call(main_kernel, in_specs=[smem, smem, vmem, hbm, hbm], out_sp...]
where the time goes in v7:
time: 105 us
  Pallas kernels  99.9 us (95%)
  other arithmetic  3.59 us (3%)
  local copies, waits for them, and re-layouts  1.61 us (2%)
    pallas_call x1, Pallas kernels, exchange(): pl.pallas_call(main_kernel, in_specs=[smem, smem, vmem, hbm, hbm], out_sp...  99.9 us

profile of v7, /device:TPU:2, one launch (start us, length us, event | category | flops | bytes accessed | tf_op | source)
XLA Modules:
  0.0 105.1 jit_solution(2747629751221996395)
XLA Ops:
  0.0 0.7 fusion.1
  0.7 0.1 and.49
  0.8 0.7 broadcast_subtract_fusion
  1.5 0.1 sub.23
  1.6 0.1 div.21
  1.7 0.6 convert_reduce_fusion
  2.3 0.8 select_reduce_fusion
  3.1 0.8 select_reduce_fusion.1
  3.8 99.9 %exchange.1 = f32[64,128]{1,0:T(8,128)} custom-call(s32[6,16]{1,0:T(8,128)} %bitcast.8, s32[6,16]{1,0:T(8,128)} %bitcast.9, f32[1,12288]{1,0:T(1,128)} %bitcast.7, bf16[64,12288]{1,0:T(8,128)(2,1)} %a_hbm.1, bf16[128,12288]{1,0:T(8,128)(2,1)} %p_hbm.1), custom_call_target="tpu_custom_call" | custom-call | tf_op jit(solution)/shard_map/exchange/pallas_call | solution.py:296
  103.7 1.4 %copy.6 = f32[64,128]{1,0:T(8,128)} copy(f32[64,128]{1,0:T(8,128)} %exchange.1) | data formatting | bytes 65536
  (5 shorter events, 0.0 us)

commit v8 on v6

--- a/solution.py
+++ b/solution.py
@@ -214,35 +214,27 @@
             acc = acc + zrecv[slot, frm].astype(jnp.float32)
         return acc
 
-    arrived(pfin.at[0], rsp.at[0])
-    arrived(pfin.at[1], rsp.at[1])
-    for l in range(2):
+    def pair(base, l):
         for h in range(2):
-            v = times(lhs(h, l), pfin[0:2].reshape(256, KLOC))
-            for slot in range(2):
-                w = v[:, slot * 128:(slot + 1) * 128]
+            v = times(lhs(h, l), pfin[base:base + 2].reshape(256, KLOC))
+            for slot in (base, base + 1):
+                w = v[:, (slot - base) * 128:(slot - base + 1) * 128]
                 if l == 0:
                     ysend[slot, h] = w.astype(ysend.dtype)
                     over_y(slot, h).start()
                 else:
                     keep[slot, h] = w
 
-    def one(slot):
-        arrived(pfin.at[slot], rsp.at[slot])
-        for l in range(2):
-            for h in range(2):
-                w = times(lhs(h, l), pfin[slot])
-                if l == 0:
-                    ysend[slot, h] = w.astype(ysend.dtype)
-                    over_y(slot, h).start()
-                else:
-                    keep[slot, h] = w
-
-    one(2)
-    for slot in (1, 0, 2):
-        to_z(slot)
-    one(3)
+    for base in (0, 2):
+        arrived(pfin.at[base], rsp.at[base])
+        arrived(pfin.at[base + 1], rsp.at[base + 1])
+        pair(base, 0)
+    pair(0, 1)
+    to_z(1)
+    to_z(0)
+    pair(2, 1)
     to_z(3)
+    to_z(2)
     for slot in (1, 2):
         xsend[slot - 1] = summed(slot)
         over_x(slot).start()

time: 96.5 us -> 96.9 us (level)
  no operation moved by 1% of the time
where the time goes in v8:
time: 96.9 us; the launch traced here: 96.6 us
  Pallas kernels  91.4 us (94%)
  other arithmetic  3.59 us (4%)
  local copies, waits for them, and re-layouts  1.61 us (2%)
    pallas_call x1, Pallas kernels, exchange(): pl.pallas_call(main_kernel, in_specs=[smem, smem, vmem, hbm, hbm], out_sp...  91.4 us

profile of v8, /device:TPU:2, one launch (start us, length us, event | category | flops | bytes accessed | tf_op | source)
XLA Modules:
  0.0 96.6 jit_solution(2161772202379706513)
XLA Ops:
  0.0 0.7 fusion.1
  0.7 0.1 and.49
  0.8 0.7 broadcast_subtract_fusion
  1.5 0.1 sub.23
  1.6 0.1 div.21
  1.7 0.6 convert_reduce_fusion
  2.3 0.8 select_reduce_fusion
  3.1 0.8 select_reduce_fusion.1
  3.8 91.4 %exchange.1 = f32[64,128]{1,0:T(8,128)} custom-call(s32[6,16]{1,0:T(8,128)} %bitcast.8, s32[6,16]{1,0:T(8,128)} %bitcast.9, f32[1,12288]{1,0:T(1,128)} %bitcast.7, bf16[64,12288]{1,0:T(8,128)(2,1)} %a_hbm.1, bf16[128,12288]{1,0:T(8,128)(2,1)} %p_hbm.1), custom_call_target="tpu_custom_call" | custom-call | tf_op jit(solution)/shard_map/exchange/pallas_call | solution.py:275
  95.3 1.4 %copy.6 = f32[64,128]{1,0:T(8,128)} copy(f32[64,128]{1,0:T(8,128)} %exchange.1) | data formatting | bytes 65536
  (5 shorter events, 0.0 us)

commit v9 on v8

--- a/solution.py
+++ b/solution.py
@@ -87,6 +87,23 @@
         span = slice(i * PEN, (i + 1) * PEN)
         p3[i] = (p_v[:, span].astype(jnp.float32) * w_ref[:, span]).astype(jnp.bfloat16)
 
+    def p_copy(slot):
+        d = XORDER[slot - 1]
+        return remote(psort.at[d], pfin.at[XORDER.index(NX - d) + 1], ssp.at[slot - 1],
+                      rsp.at[XORDER.index(NX - d) + 1], device(z, ylo, yh, (x + d) % NX, c))
+
+    own_p = pltpu.make_async_copy(psort.at[0], pfin.at[0], rsp.at[0])
+    def sort_p(d):
+        for zi in range(2):
+            dz = (x + d) % NX + NX * zi
+            for ls in range(2):
+                src = ((z - dz + NZ) % NZ) * 2 + ls
+                for r in range(SHARE):
+                    at = ((zi * 2 + ls) * SHARE + r) * PEN
+                    psort[d, :, at:at + PEN] = p3[idx_p[r, src]]
+
+    sort_p(1)
+
     pl.semaphore_wait(bar, 7 + 3 + 3 + 1 + 7 + (x + NX - 1) // NX)
 
     def a_copy(h, dz, l):
@@ -94,7 +111,7 @@
         return remote(asort.at[dz, lt, h], r1.at[dz // NX, x, lt, h], ss1.at[dz, l, h],
                       rs1.at[dz // NX, x, lt, h], device((z + dz) % NZ, ylo, yh, dz % NX, c))
 
-    for h in range(2):
+    def send_a(h):
         for dz in ORDER:
             for l in range(2):
                 if dz == 0:
@@ -110,24 +127,15 @@
                 else:
                     a_copy(h, dz, l).start()
 
-    def p_copy(slot):
-        d = XORDER[slot - 1]
-        return remote(psort.at[d], pfin.at[XORDER.index(NX - d) + 1], ssp.at[slot - 1],
-                      rsp.at[XORDER.index(NX - d) + 1], device(z, ylo, yh, (x + d) % NX, c))
-
-    own_p = pltpu.make_async_copy(psort.at[0], pfin.at[0], rsp.at[0])
-    for step, d in enumerate(XORDER + (0,)):
-        for zi in range(2):
-            dz = (x + d) % NX + NX * zi
-            for ls in range(2):
-                src = ((z - dz + NZ) % NZ) * 2 + ls
-                for r in range(SHARE):
-                    i = idx_p[r, src]
-                    at = ((zi * 2 + ls) * SHARE + r) * PEN
-                    psort[d, :, at:at + PEN] = p3[i]
-        if step >= 1:
-            p_copy(step).start()
+    p_copy(1).start()
+    send_a(0)
+    sort_p(3)
+    sort_p(2)
+    p_copy(2).start()
+    sort_p(0)
+    p_copy(3).start()
     own_p.start()
+    send_a(1)
 
     flip = x // 3
     chunks = [(h, j, d, l) for h in range(2) for j in range(2) for d in (0, 1, 3, 2) for l in range(2)]

time: 96.9 us -> 115 us (1.19)
  the two profiles are of different devices: /device:TPU:2 before, /device:TPU:4 now
where the time goes in v9:
time: 115 us
  Pallas kernels  110 us (96%)
  other arithmetic  3.59 us (3%)
  local copies, waits for them, and re-layouts  1.61 us (1%)
    pallas_call x1, Pallas kernels, exchange(): pl.pallas_call(main_kernel, in_specs=[smem, smem, vmem, hbm, hbm], out_sp...  110 us

profile of v9, /device:TPU:4, one launch (start us, length us, event | category | flops | bytes accessed | tf_op | source)
XLA Modules:
  0.0 114.8 jit_solution(2221827039114359344)
XLA Ops:
  0.0 0.7 fusion.1
  0.7 0.1 and.49
  0.8 0.7 broadcast_subtract_fusion
  1.5 0.1 sub.23
  1.6 0.1 div.21
  1.7 0.6 convert_reduce_fusion
  2.3 0.8 select_reduce_fusion
  3.1 0.8 select_reduce_fusion.1
  3.8 109.6 %exchange.1 = f32[64,128]{1,0:T(8,128)} custom-call(s32[6,16]{1,0:T(8,128)} %bitcast.8, s32[6,16]{1,0:T(8,128)} %bitcast.9, f32[1,12288]{1,0:T(1,128)} %bitcast.7, bf16[64,12288]{1,0:T(8,128)(2,1)} %a_hbm.1, bf16[128,12288]{1,0:T(8,128)(2,1)} %p_hbm.1), custom_call_target="tpu_custom_call" | custom-call | tf_op jit(solution)/shard_map/exchange/pallas_call | solution.py:283
  113.4 1.4 %copy.6 = f32[64,128]{1,0:T(8,128)} copy(f32[64,128]{1,0:T(8,128)} %exchange.1) | data formatting | bytes 65536
  (5 shorter events, 0.0 us)
